TPU v7x, 128 devices: a whole 4x4x4 slice. The times are simulated.
128 devices in a mesh: obs: 4 (over z_hi, core), par: 32 (over y, x, z_lo).
Axes of the slice: x: 4, y: 4, z: 4 (z_hi: 2, z_lo: 2; z = z_hi * 2 + z_lo), core: 2. Of those that a mesh axis runs over, the one named last changes fastest.
Arguments:
- jacobian: bfloat16 [3072, 16384], P(('obs', 'par')), may hold values from -0.109375 to 0.109375
- obs_weights: float32 [3072], replicated, may hold values from 0.1 to 10
- time_to_obs: int32 [3072], P(('obs', 'par')), may hold values from 0 to 3071, each once
Outputs:
- normal_matrix: float32 [16384, 16384], P('obs', 'par')
Inputs may be any that keep to these rules, and one draw needn't show every extreme that they name: `time_to_obs`: each observation index appears exactly once.
All inputs are finite; a program needn't handle non-finite values.
Results may differ from a plain program's by a relative error of at most 0.0039.
Values may be sent and summed in bfloat16 or wider, within the bound.
No kernel may reach another device: no remote copies, remote signals or barrier semaphores. Data moves between devices by JAX's collectives and lax.ppermute only.
A program may use at most 128 MiB of HBM per device.

v0:
```python
import jax
import jax.numpy as jnp
from jax import lax
from jax.sharding import PartitionSpec as P


def on_device(jacobian, obs_weights, time_to_obs):
    rows_here = jacobian.shape[0]
    param_count = jacobian.shape[1]
    obs_count = lax.axis_size("obs")
    par_count = lax.axis_size("par")
    indices = jnp.arange(obs_weights.shape[0], dtype=jnp.int32)
    picked = jnp.sum(
        jnp.where(time_to_obs[:, None] == indices[None, :], obs_weights[None, :], 0.0), axis=1
    )
    scaled = (jnp.sqrt(picked)[:, None] * jacobian.astype(jnp.float32)).astype(jnp.bfloat16)
    lifted = scaled.reshape(1, rows_here, param_count)
    blocks = lax.all_to_all(lifted, "obs", split_axis=2, concat_axis=0, tiled=True)
    col_width = param_count // par_count
    columns = lax.all_to_all(lifted, "par", split_axis=2, concat_axis=0, tiled=True)
    columns = lax.all_gather(columns, "obs", axis=0, tiled=True)
    columns = columns.reshape(obs_count, par_count * rows_here, col_width)
    panels = lax.all_gather(blocks, "par", axis=1, tiled=True)
    return jnp.einsum("arc,ard->cd", panels, columns, preferred_element_type=jnp.float32)


def solution(mesh):
    placed = (P(("obs", "par"), None), P(), P(("obs", "par")))
    return jax.shard_map(
        on_device, mesh=mesh, in_specs=placed, out_specs=P("obs", "par"), check_vma=False
    )
```

profile of v0, /device:TPU:1, one launch (start us, length us, event | category | flops | bytes accessed | tf_op | source)
XLA Modules:
  0.0 776.0 jit_solution(6125067894253872118)
XLA Ops:
  6.5 0.9 select_reduce_fusion
  7.5 1.3 fusion.5
  8.8 12.5 %copy.17 = bf16[1,24,16384]{1,0,2:T(2,128)(2,1)} copy(bf16[1,24,16384]{2,1,0:T(8,128)(2,1)S(1)} %fusion.5) | data formatting | bytes 1572864 | tf_op jit(solution)/shard_map/reshape | solution.py:17
  21.3 0.5 broadcast.2
  21.8 90.6 %reduce.1 = bf16[16384,24]{1,0:T(8,128)(2,1)} reduce(bf16[16384,1,24]{2,1,0:T(2,128)(2,1)} %bitcast.26, bf16[]{:T(256)} %broadcast.2), dimensions={1}, to_apply=%bitcast.22.reduce_sub_computation | reduce | bytes 1572866
  112.5 6.6 reshape.19
  119.1 18.6 %all_to_all.36 = bf16[4,2,49152]{2,1,0:T(2,128)(2,1)S(1)} all-to-all(bf16[4,2,49152]{2,1,0:T(2,128)(2,1)S(1)} %reshape.19), channel_id=1, replica_groups=mesh['obs'=4,'par'=32] {'obs'}, dimensions={0} | all-to-all | bytes 1572864 | tf_op jit(solution)/shard_map/all_to_all | solution.py:18
  137.6 12.0 %reshape.20 = bf16[16384,1,24]{2,1,0:T(2,128)(2,1)} reshape(bf16[4,2,49152]{2,1,0:T(2,128)(2,1)S(1)} %all_to_all.36) | data formatting | bytes 1572864
  149.7 15.2 %copy.18 = bf16[1,24,16384]{2,1,0:T(8,128)(2,1)S(1)} copy(bf16[1,24,16384]{1,0,2:T(2,128)(2,1)} %bitcast.28) | data formatting | bytes 1572864 | tf_op jit(solution)/shard_map/all_to_all | solution.py:18
  164.8 1.5 all_to_all.27
  166.3 0.0 all-gather.5.cloned.1.call-update
  166.4 0.2 all-gather.7.cloned.1.call-start
  166.6 90.7 %reduce = bf16[16384,24]{1,0:T(8,128)(2,1)} reduce(bf16[16384,1,24]{2,1,0:T(2,128)(2,1)} %bitcast.27, bf16[]{:T(256)} %broadcast.2), dimensions={1}, to_apply=%bitcast.20.reduce_sub_computation | reduce | bytes 1572866
  257.3 7.4 reshape.17
  264.6 22.5 %all_to_all.37 = bf16[32,2,6144]{2,1,0:T(2,128)(2,1)S(1)} all-to-all(bf16[32,2,6144]{2,1,0:T(2,128)(2,1)S(1)} %reshape.17), channel_id=1, replica_groups=mesh['obs'=4,'par'=32] {'par'}, dimensions={0} | all-to-all | bytes 1572864 | tf_op jit(solution)/shard_map/all_to_all | solution.py:20
  287.2 17.3 %reshape.18 = bf16[16384,1,24]{2,1,0:T(2,128)(2,1)} reshape(bf16[32,2,6144]{2,1,0:T(2,128)(2,1)S(1)} %all_to_all.37) | data formatting | bytes 1572864
  304.5 15.2 %copy.22 = bf16[1,24,16384]{2,1,0:T(8,128)(2,1)S(1)} copy(bf16[1,24,16384]{1,0,2:T(2,128)(2,1)} %bitcast.29) | data formatting | bytes 1572864 | tf_op jit(solution)/shard_map/all_to_all | solution.py:20
  319.7 0.2 copy.24
  320.0 0.1 bitcast_bitcast_fusion
  320.1 1.3 copy.23
  321.4 0.0 all-gather.7.cloned.1.call-update
  321.4 387.8 %all-gather.5.cloned.1.call-done = bf16[4,1,768,4096]{3,0,1,2:T(4,128)(2,1)} async-done(((bf16[4,1,24,4096]{3,0,1,2:T(4,128)(2,1)}), bf16[4,1,768,4096]{3,0,1,2:T(4,128)(2,1)}) %all-gather.5.cloned.1.call-update) | async-done | bytes 25165840 | tf_op jit(solution)/shard_map/all_gather | solution.py:23
  709.2 39.0 %copy.20 = bf16[4,1,768,4096]{2,3,0,1:T(8,128)(2,1)} copy(bf16[4,1,768,4096]{3,0,1,2:T(4,128)(2,1)} %all-gather.5.cloned.1.call-done) | data formatting | bytes 50331648 | tf_op jit(solution)/shard_map/all_gather | solution.py:23
  748.2 20.9 %fusion.2 = f32[4096,512]{1,0:T(8,128)} fusion(bf16[4,768,512]{2,1,0:T(8,128)(2,1)} %bitcast.33, bf16[4,1,768,4096]{2,3,0,1:T(8,128)(2,1)} %copy.20), kind=kOutput, calls=%fused_computation.2 | convolution fusion | flops 12884901888 | bytes 36700160 | tf_op jit(solution)/shard_map/arc,ard->cd/dot_general | solution.py:24
  (3 shorter events, 0.0 us)
Async XLA Ops:
  6.5 702.7 %all-gather.5.cloned.1.call-start = ((), (), s32[]{:S(2)}) async-start(), calls=%async_computation.2 | async-start | bytes 25952256 | tf_op jit(solution)/shard_map/all_gather | solution.py:23
  166.4 581.8 %all-gather.7.cloned.1.call-start = ((), (), s32[]{:S(2)}) async-start(), calls=%async_computation.3 | async-start | bytes 3932160 | tf_op jit(solution)/shard_map/all_gather | solution.py:21
Sparse Core Ops, SparseCore 0:
  166.5 542.6 all-gather.4
  710.9 34.5 all-gather.6
where the time goes:
time: 779 us; the launch traced here: 776 us
  waiting for transfers between devices  388 us (50%)
  other arithmetic  184 us (24%)
  local copies, waits for them, and re-layouts  129 us (17%)
  blocking collectives  41.1 us (5%)
  matrix products  20.9 us (3%)
  between operations  13.5 us (2%)
    all_gather x1, waiting for transfers between devices, on_device(): panels = lax.all_gather(blocks, 'par', axis=1, tiled=True)  388 us
    unnamed x2, other arithmetic  181 us
    unnamed x6, local copies, waits for them, and re-layouts  44.1 us
    all_gather x1, local copies, waits for them, and re-layouts, on_device(): panels = lax.all_gather(blocks, 'par', axis=1, tiled=True)  39 us
    all_to_all x1, blocking collectives, on_device(): lax.all_to_all(lifted, 'par', split_axis=2, concat_axis=0, tiled=True)  22.5 us
    dot_general x1, matrix products, on_device(): jnp.einsum('arc,ard->cd', panels, columns, preferred_element_type=jnp.flo...  20.9 us
    all_to_all x1, blocking collectives, on_device(): lax.all_to_all(lifted, 'obs', split_axis=2, concat_axis=0, tiled=True)  18.6 us
    all_to_all x2, local copies, waits for them, and re-layouts, on_device(): lax.all_to_all(lifted, 'obs', split_axis=2, concat_axis=0, tiled=True)  16.7 us
  transfers between devices with their start and end apart: 2, of which 1 were waited for; matrix products, arithmetic and copies ran while one was open for 22% of the time, Pallas kernels for 0%

commit v1 on v0

v1 whole, which is shorter than its diff:
```python
import itertools

import jax
import jax.numpy as jnp
from jax import lax
from jax.experimental import pallas as pl
from jax.experimental.pallas import tpu as pltpu
from jax.sharding import Mesh
from jax.sharding import PartitionSpec as P

NAMES = ("zh", "c", "y", "x", "zl")
SIZES = (2, 2, 4, 4, 2)
CHUNKS = 4
VMEM = 56 * 1024 * 1024


def z_shift(value, step):
    return lax.ppermute(value, ("zh", "zl"), [(z, (z + step) % 4) for z in range(4)])


def ring_shift(value, step, ring):
    table = []
    for c, y, x in itertools.product(range(2), range(4), range(4)):
        if c == ring:
            to = (c, y, (x + step) % 4)
        else:
            to = (c, (y + step) % 4, x)
        table.append(((c * 4 + y) * 4 + x, (to[0] * 4 + to[1]) * 4 + to[2]))
    return lax.ppermute(value, ("c", "y", "x"), table)


def whole(shape):
    return pl.BlockSpec(shape, lambda: (0,) * len(shape))


def in_vmem(kernel, outs, *args):
    return pl.pallas_call(
        kernel,
        out_shape=outs,
        in_specs=[
            pl.BlockSpec(memory_space=pltpu.SMEM)
            if a.dtype == jnp.int32 else whole(a.shape)
            for a in args
        ],
        out_specs=jax.tree.map(lambda o: whole(o.shape), outs),
        compiler_params=pltpu.CompilerParams(vmem_limit_bytes=VMEM),
    )(*args)


def shape_of(rows, cols, dtype=jnp.bfloat16):
    return jax.ShapeDtypeStruct((rows, cols), dtype)


def split_rows(place, jacobian, root):
    rows, params = jacobian.shape
    quarter, wide, half = params // 4, params // 16, params // 32

    def kernel(place_ref, jac_ref, root_ref, *outs):
        scale = root_ref[...]
        z, c, a = place_ref[0], place_ref[1], place_ref[2]
        for n, step in enumerate((0, 1, 3, 2)):
            at = pl.multiple_of(lax.rem(z + step, 4) * quarter, quarter)
            piece = jac_ref[:, pl.ds(at, quarter)].astype(jnp.float32)
            outs[n][...] = (scale * piece).astype(jnp.bfloat16)
        for n, step in enumerate((0, 1, 3, 2)):
            block = lax.rem(a + step, 4)
            for j in range(4):
                first = jnp.where(c == 0, 4 * j + block, 4 * block + j) * 2
                for h in range(2):
                    own = jnp.where(c == 0, h, 1 - h)
                    at = pl.multiple_of((first + own) * half, half)
                    piece = jac_ref[:, pl.ds(at, half)].astype(jnp.float32)
                    outs[4 + n][:, j * wide + h * half : j * wide + (h + 1) * half] = (
                        scale * piece
                    ).astype(jnp.bfloat16)

    return in_vmem(kernel, [shape_of(rows, quarter)] * 8, place, jacobian, root)


def regroup_columns(place, pieces):
    rows, quarter = pieces[0].shape
    wide = quarter // 4

    def kernel(place_ref, *refs):
        b = place_ref[3]
        for n, step in enumerate((0, 1, 3, 2)):
            at = pl.multiple_of(lax.rem(b + step, 4) * wide, wide)
            for i in range(4):
                refs[4 + n][i * rows : (i + 1) * rows, :] = refs[i][:, pl.ds(at, wide)]

    return in_vmem(kernel, [shape_of(4 * rows, wide)] * 4, place, *pieces)


def stack_chunks(pieces, widths):
    rows = [p.shape[0] for p in pieces]

    def kernel(*refs):
        outs = refs[len(pieces) :]
        at = 0
        for out, width in zip(outs, widths):
            top = 0
            for piece, n in zip(refs, rows):
                out[top : top + n, :] = piece[:, at : at + width]
                top += n
            at += width

    return in_vmem(kernel, [shape_of(sum(rows), w) for w in widths], *pieces)


def products(pieces, columns):
    width, half = pieces[0].shape[1], columns.shape[1] // 2
    block = min(256, width)

    def kernel(*refs):
        rows = jnp.concatenate([r[...] for r in refs[: len(pieces)]], axis=0)
        total = lax.dot_general(
            rows, refs[len(pieces)][...], (((0,), (0,)), ((), ())), preferred_element_type=jnp.float32
        )
        refs[-2][...] = total[:, :half]
        refs[-1][...] = total[:, half:]

    return pl.pallas_call(
        kernel,
        grid=(width // block,),
        in_specs=[pl.BlockSpec((p.shape[0], block), lambda i: (0, i)) for p in pieces]
        + [pl.BlockSpec(columns.shape, lambda i: (0, 0))],
        out_specs=[pl.BlockSpec((block, half), lambda i: (i, 0))] * 2,
        out_shape=[shape_of(width, half, jnp.float32)] * 2,
        compiler_params=pltpu.CompilerParams(vmem_limit_bytes=VMEM),
    )(*pieces, columns)


def on_device(jacobian, obs_weights, time_to_obs):
    rows, params = jacobian.shape
    quarter, wide = params // 4, params // 16
    zh, c, y, x, zl = (lax.axis_index(n) for n in NAMES)
    a = jnp.where(c == 0, x, y)
    b = jnp.where(c == 0, y, x)
    place = jnp.stack([2 * zh + zl, c, a, b]).astype(jnp.int32)

    indices = jnp.arange(obs_weights.shape[0], dtype=jnp.int32)
    picked = jnp.sum(
        jnp.where(time_to_obs[:, None] == indices[None, :], obs_weights[None, :], 0.0), axis=1
    )
    cut = split_rows(place, jacobian, jnp.sqrt(picked)[:, None])

    first = [cut[4]] + [ring_shift(cut[4 + n], s, 0) for n, s in ((1, 1), (2, -1), (3, 2))]
    groups = regroup_columns(place, first)
    second = [groups[0]] + [ring_shift(groups[n], s, 1) for n, s in ((1, 1), (2, -1), (3, 2))]
    flat = jnp.concatenate(second, axis=0)
    back = z_shift(flat, 1)
    front = z_shift(flat, -1)
    mid = flat.shape[0] // 2
    far = [z_shift(back[:mid], 1), z_shift(front[mid:], -1)]
    columns = jnp.stack([flat, back, front, jnp.concatenate(far, axis=0)])
    columns = columns.reshape(4, 16, rows, wide).transpose(1, 0, 2, 3).reshape(64 * rows, wide)

    column = jnp.concatenate(
        [cut[0]] + [z_shift(cut[n], s) for n, s in ((1, 1), (2, -1), (3, 2))], axis=0
    )
    ring = [column] + [ring_shift(column, s, 0) for s in (1, -1, 2)]
    widths = [quarter // CHUNKS] * CHUNKS
    done = []
    for group in stack_chunks(ring, widths):
        back = ring_shift(group, 1, 1)
        front = ring_shift(group, -1, 1)
        mid = group.shape[0] // 2
        far = [ring_shift(back[:mid], 1, 1), ring_shift(front[mid:], -1, 1)]
        mine, other = products([group, back, front] + far, columns)
        mine = mine + lax.ppermute(other, "c", [(0, 1), (1, 0)])
        moved = lax.ppermute(mine.astype(jnp.bfloat16), ("c", "zl"), [(1, 2), (2, 1)])
        done.append(jnp.where(c == zl, mine, moved.astype(jnp.float32)))
    return jnp.concatenate(done, axis=0)


def solution(mesh):
    fine = Mesh(mesh.devices.reshape(SIZES), NAMES)
    rows = ("zh", "c", "y", "x", "zl")
    return jax.shard_map(
        on_device,
        mesh=fine,
        in_specs=(P(rows, None), P(), P(rows)),
        out_specs=P(("zh", "c"), ("y", "x", "zl")),
        check_vma=False,
    )
```

time: 779 us -> 211 us (0.27)
  waiting for transfers between devices: 388 us -> 78 us
  other arithmetic: 184 us -> 17.9 us
  local copies, waits for them, and re-layouts: 129 us -> 10.9 us
  starting transfers between devices: 0.22 us -> 63.6 us
  blocking collectives: 41.1 us -> 0 us
  Pallas kernels: 0 us -> 39.3 us
  matrix products: 20.9 us -> 0 us
  between operations: 13.5 us -> 0.45 us
    all_gather x2 -> x0, waiting for transfers between devices: 388 us -> none  [the longest x1 388 us: on_device(): panels = lax.all_gather(blocks, 'par', axis=1, tiled=True)]
    unnamed x2 -> x0, other arithmetic: 181 us -> none
    ppermute x0 -> x40, waiting for transfers between devices: none -> 78 us  [the longest x25 44.1 us: ring_shift(): return lax.ppermute(value, ('c', 'y', 'x'), table)]
    ppermute x0 -> x40, starting transfers between devices: none -> 63.6 us  [the longest x25 33.2 us: ring_shift(): return lax.ppermute(value, ('c', 'y', 'x'), table)]
    all_to_all x2 -> x0, blocking collectives: 41.1 us -> none  [the longest x1 22.5 us: on_device(): lax.all_to_all(lifted, 'par', split_axis=2, concat_axis=0, tiled=True)]
    pallas_call x0 -> x7, Pallas kernels: none -> 39.3 us  [the longest x4 31 us: products(): pl.pallas_call(kernel, grid=(width // block,), in_specs=[pl.BlockSpec((p....]
    all_gather x1 -> x0, local copies, waits for them, and re-layouts: 39 us -> none  [on_device(): panels = lax.all_gather(blocks, 'par', axis=1, tiled=True)]
    unnamed x6 -> x62, local copies, waits for them, and re-layouts: 44.1 us -> 8.34 us
  transfers between devices with their start and end apart: 2 -> 40, of which waited for: 1 -> 13; matrix products, arithmetic and copies ran while one was open for 22% -> 8% of each run, Pallas kernels for 0% -> 18%
where the time goes in v1:
time: 211 us; the launch traced here: 210 us
  waiting for transfers between devices  78 us (37%)
  starting transfers between devices  63.6 us (30%)
  Pallas kernels  39.3 us (19%)
  other arithmetic  17.9 us (8%)
  local copies, waits for them, and re-layouts  10.9 us (5%)
    ppermute x25, waiting for transfers between devices, ring_shift(): return lax.ppermute(value, ('c', 'y', 'x'), table)  44.1 us
    ppermute x25, starting transfers between devices, ring_shift(): return lax.ppermute(value, ('c', 'y', 'x'), table)  33.2 us
    pallas_call x4, Pallas kernels, products(): pl.pallas_call(kernel, grid=(width // block,), in_specs=[pl.BlockSpec((p....  31 us
    ppermute x4, waiting for transfers between devices, on_device(): lax.ppermute(mine.astype(jnp.bfloat16), ('c', 'zl'), [(1, 2), (2, 1)])  30.8 us
    ppermute x4, starting transfers between devices, on_device(): lax.ppermute(mine.astype(jnp.bfloat16), ('c', 'zl'), [(1, 2), (2, 1)])  11.1 us
    ppermute x7, starting transfers between devices, z_shift(): lax.ppermute(value, ('zh', 'zl'), [(z, (z + step) % 4) for z in range(4)])  10.1 us
    ppermute x4, starting transfers between devices, on_device(): mine = mine + lax.ppermute(other, 'c', [(0, 1), (1, 0)])  9.15 us
    convert_element_type x4, other arithmetic, on_device(): mine.astype(jnp.bfloat16)  9.03 us
  transfers between devices with their start and end apart: 40, of which 13 were waited for; matrix products, arithmetic and copies ran while one was open for 8% of the time, Pallas kernels for 18%

profile of v1, /device:TPU:1, one launch (start us, length us, event | category | flops | bytes accessed | tf_op | source)
XLA Modules:
  0.0 210.1 jit_solution(13620939504160573869)
XLA Ops:
  20.2 3.1 %collective-permute-done.2 = bf16[24,4096]{1,0:T(8,128)(2,1)S(1)} collective-permute-done((bf16[24,4096]{1,0:T(8,128)(2,1)}, bf16[24,4096]{1,0:T(8,128)(2,1)S(1)}, u32[]{:S(2)}, u32[]{:S(2)}) %collective-permute-start.2) | collective-permute-done | bytes 196640 | tf_op jit(solution)/shard_map/ppermute | solution.py:18
  26.1 3.7 %collective-permute-start.14 = (bf16[96,1024]{1,0:T(8,128)(2,1)}, bf16[96,1024]{1,0:T(8,128)(2,1)S(1)}, u32[]{:S(2)}, u32[]{:S(2)}) collective-permute-start(bf16[96,1024]{1,0:T(8,128)(2,1)} %get-tuple-element.40), channel_id=1, source_target_pairs={{0,24},{2,26},{4,28},{6,30},{8,0},{10,2},{12,4},{14,6},{16,8},{18,... | collective-permute-start | bytes 589832 | tf_op jit(solution)/shard_map/ppermute | solution.py:29
  30.8 6.0 %collective-permute-done.14 = bf16[96,1024]{1,0:T(8,128)(2,1)S(1)} collective-permute-done((bf16[96,1024]{1,0:T(8,128)(2,1)}, bf16[96,1024]{1,0:T(8,128)(2,1)S(1)}, u32[]{:S(2)}, u32[]{:S(2)}) %collective-permute-start.14) | collective-permute-done | bytes 196640 | tf_op jit(solution)/shard_map/ppermute | solution.py:29
  42.3 4.5 %collective-permute-done.3.refs_1_ = bf16[96,4096]{1,0:T(8,128)(2,1)S(1)} collective-permute-done((bf16[96,4096]{1,0:T(8,128)(2,1)S(1)}, bf16[96,4096]{1,0:T(8,128)(2,1)S(1)}, u32[]{:S(2)}, u32[]{:S(2)}) %collective-permute-start.3) | collective-permute-done | bytes 786464 | tf_op jit(solution)/shard_map/ppermute | solution.py:29
  49.5 3.7 %shard_map.38 = (bf16[384,1024]{1,0:T(8,128)(2,1)}, bf16[384,1024]{1,0:T(8,128)(2,1)}, bf16[384,1024]{1,0:T(8,128)(2,1)}, bf16[384,1024]{1,0:T(8,128)(2,1)}) custom-call(bf16[96,4096]{1,0:T(8,128)(2,1)} %copy-done.12, bf16[96,4096]{1,0:T(8,128)(2,1)} %copy-done.15, bf16[96,4096]{1,0:T(8,128)(2,1)} %copy-done.16, bf16[96,4096]{1,0:T(8,128)(2,1)} %copy-done.17), custom_call_target="tpu_custom_call" | custom-call | tf_op jit(solution)/shard_map/pallas_call | solution.py:37
  60.4 6.3 %collective-permute-done.6.refs_1_ = bf16[384,1024]{1,0:T(8,128)(2,1)S(1)} collective-permute-done((bf16[384,1024]{1,0:T(8,128)(2,1)}, bf16[384,1024]{1,0:T(8,128)(2,1)S(1)}, u32[]{:S(2)}, u32[]{:S(2)}) %collective-permute-start.6) | collective-permute-done | bytes 786464 | tf_op jit(solution)/shard_map/ppermute | solution.py:29
  68.4 6.8 %collective-permute-done.22.refs_1_ = bf16[384,1024]{1,0:T(8,128)(2,1)S(1)} collective-permute-done((bf16[384,1024]{1,0:T(8,128)(2,1)}, bf16[384,1024]{1,0:T(8,128)(2,1)S(1)}, u32[]{:S(2)}, u32[]{:S(2)}) %collective-permute-start.22) | collective-permute-done | bytes 786464 | tf_op jit(solution)/shard_map/ppermute | solution.py:29
  85.1 6.7 %collective-permute-done.9.refs_4_ = bf16[192,1024]{1,0:T(8,128)(2,1)S(1)} collective-permute-done((bf16[192,1024]{1,0:T(8,128)(2,1)S(1)}, bf16[192,1024]{1,0:T(8,128)(2,1)S(1)}, u32[]{:S(2)}, u32[]{:S(2)}) %collective-permute-start.9) | collective-permute-done | bytes 393248 | tf_op jit(solution)/shard_map/ppermute | solution.py:29
  92.6 7.8 %shard_map.40 = (f32[1024,512]{1,0:T(8,128)}, f32[1024,512]{1,0:T(8,128)}) custom-call(bf16[384,1024]{1,0:T(8,128)(2,1)} %get-tuple-element.33.refs_0_, bf16[384,1024]{1,0:T(8,128)(2,1)} %copy-done.8, bf16[384,1024]{1,0:T(8,128)(2,1)} %copy-done.9, bf16[192,1024]{1,0:T(8,128)(2,1)} %copy-done.19, bf16[192,1024]{1,0:T(8,128)(2,1)} %copy-done.21, ...), custom_call_target="tpu_custom_call" | custom-call | tf_op jit(solution)/shard_map/pallas_call | solution.py:122
  100.4 5.2 %collective-permute-start.20 = (f32[1024,512]{1,0:T(8,128)}, f32[1024,512]{1,0:T(8,128)}, u32[]{:S(2)}, u32[]{:S(2)}) collective-permute-start(f32[1024,512]{1,0:T(8,128)} %get-tuple-element.43), channel_id=1, source_target_pairs={{0,32},{32,0},{1,33},{33,1},{2,34},{34,2},{3,35},{35,3},{4,36},{36... | collective-permute-start | bytes 6291464 | tf_op jit(solution)/shard_map/ppermute | solution.py:170
  108.8 7.7 %shard_map.41 = (f32[1024,512]{1,0:T(8,128)}, f32[1024,512]{1,0:T(8,128)}) custom-call(bf16[384,1024]{1,0:T(8,128)(2,1)} %get-tuple-element.44.refs_0_, bf16[384,1024]{1,0:T(8,128)(2,1)} %copy-done.4, bf16[384,1024]{1,0:T(8,128)(2,1)} %copy-done.5, bf16[192,1024]{1,0:T(8,128)(2,1)} %copy-done.18, bf16[192,1024]{1,0:T(8,128)(2,1)} %collective-permute-done.25.refs_4_, ...), custom_call_target="tpu_custom_call" | custom-call | tf_op jit(solution)/shard_map/pallas_call | solution.py:122
  119.7 4.8 %collective-permute-done.31.refs_4_ = bf16[192,1024]{1,0:T(8,128)(2,1)S(1)} collective-permute-done((bf16[192,1024]{1,0:T(8,128)(2,1)S(1)}, bf16[192,1024]{1,0:T(8,128)(2,1)S(1)}, u32[]{:S(2)}, u32[]{:S(2)}) %collective-permute-start.31) | collective-permute-done | bytes 393248 | tf_op jit(solution)/shard_map/ppermute | solution.py:29
  125.3 7.7 %shard_map.42 = (f32[1024,512]{1,0:T(8,128)}, f32[1024,512]{1,0:T(8,128)}) custom-call(bf16[384,1024]{1,0:T(8,128)(2,1)} %get-tuple-element.47.refs_0_, bf16[384,1024]{1,0:T(8,128)(2,1)} %copy-done.6, bf16[384,1024]{1,0:T(8,128)(2,1)} %copy-done.7, bf16[192,1024]{1,0:T(8,128)(2,1)} %copy-done.20, bf16[192,1024]{1,0:T(8,128)(2,1)} %copy-done.24, ...), custom_call_target="tpu_custom_call" | custom-call | tf_op jit(solution)/shard_map/pallas_call | solution.py:122
  135.0 2.7 %collective-permute-start.37 = (bf16[192,1024]{1,0:T(8,128)(2,1)S(1)}, bf16[192,1024]{1,0:T(8,128)(2,1)S(1)}, u32[]{:S(2)}, u32[]{:S(2)}) collective-permute-start(bf16[192,1024]{1,0:T(8,128)(2,1)S(1)} %slice.49), channel_id=1, source_target_pairs={{0,24},{2,26},{4,28},{6,30},{8,0},{10,2},{12,4},{14,6},{16,8},{18,... | collective-permute-start | bytes 1179656 | tf_op jit(solution)/shard_map/ppermute | solution.py:29
  137.7 5.3 %collective-permute-done.36.refs_3_ = bf16[192,1024]{1,0:T(8,128)(2,1)S(1)} collective-permute-done((bf16[192,1024]{1,0:T(8,128)(2,1)S(1)}, bf16[192,1024]{1,0:T(8,128)(2,1)S(1)}, u32[]{:S(2)}, u32[]{:S(2)}) %collective-permute-start.36) | collective-permute-done | bytes 393248 | tf_op jit(solution)/shard_map/ppermute | solution.py:29
  144.5 7.7 %shard_map.43 = (f32[1024,512]{1,0:T(8,128)}, f32[1024,512]{1,0:T(8,128)}) custom-call(bf16[384,1024]{1,0:T(8,128)(2,1)} %get-tuple-element.50.refs_0_, bf16[384,1024]{1,0:T(8,128)(2,1)} %copy-done.10, bf16[384,1024]{1,0:T(8,128)(2,1)} %copy-done.11, bf16[192,1024]{1,0:T(8,128)(2,1)} %copy-done.22, bf16[192,1024]{1,0:T(8,128)(2,1)} %copy-done.23, ...), custom_call_target="tpu_custom_call" | custom-call | tf_op jit(solution)/shard_map/pallas_call | solution.py:122
  156.0 2.7 %collective-permute-start.21 = (bf16[1024,512]{1,0:T(8,128)(2,1)S(1)}, bf16[1024,512]{1,0:T(8,128)(2,1)S(1)}, u32[]{:S(2)}, u32[]{:S(2)}) collective-permute-start(bf16[1024,512]{1,0:T(8,128)(2,1)S(1)} %get-tuple-element.53), channel_id=1, source_target_pairs={{1,32},{32,1},{3,34},{34,3},{5,36},{36,5},{7,38},{38,7},{9,40},{40... | collective-permute-start | bytes 3145736 | tf_op jit(solution)/shard_map/ppermute | solution.py:171
  161.0 2.9 %collective-permute-start.27 = (bf16[1024,512]{1,0:T(8,128)(2,1)S(1)}, bf16[1024,512]{1,0:T(8,128)(2,1)S(1)}, u32[]{:S(2)}, u32[]{:S(2)}) collective-permute-start(bf16[1024,512]{1,0:T(8,128)(2,1)S(1)} %get-tuple-element.55), channel_id=1, source_target_pairs={{1,32},{32,1},{3,34},{34,3},{5,36},{36,5},{7,38},{38,7},{9,40},{40... | collective-permute-start | bytes 3145736 | tf_op jit(solution)/shard_map/ppermute | solution.py:171
  166.2 2.7 %collective-permute-start.33 = (bf16[1024,512]{1,0:T(8,128)(2,1)S(1)}, bf16[1024,512]{1,0:T(8,128)(2,1)S(1)}, u32[]{:S(2)}, u32[]{:S(2)}) collective-permute-start(bf16[1024,512]{1,0:T(8,128)(2,1)S(1)} %get-tuple-element.57), channel_id=1, source_target_pairs={{1,32},{32,1},{3,34},{34,3},{5,36},{36,5},{7,38},{38,7},{9,40},{40... | collective-permute-start | bytes 3145736 | tf_op jit(solution)/shard_map/ppermute | solution.py:171
  171.0 2.9 %collective-permute-start.39 = (bf16[1024,512]{1,0:T(8,128)(2,1)S(1)}, bf16[1024,512]{1,0:T(8,128)(2,1)S(1)}, u32[]{:S(2)}, u32[]{:S(2)}) collective-permute-start(bf16[1024,512]{1,0:T(8,128)(2,1)S(1)} %get-tuple-element.59), channel_id=1, source_target_pairs={{1,32},{32,1},{3,34},{34,3},{5,36},{36,5},{7,38},{38,7},{9,40},{40... | collective-permute-start | bytes 3145736 | tf_op jit(solution)/shard_map/ppermute | solution.py:171
  174.3 9.0 %collective-permute-done.27 = bf16[1024,512]{1,0:T(8,128)(2,1)S(1)} collective-permute-done((bf16[1024,512]{1,0:T(8,128)(2,1)S(1)}, bf16[1024,512]{1,0:T(8,128)(2,1)S(1)}, u32[]{:S(2)}, u32[]{:S(2)}) %collective-permute-start.27) | collective-permute-done | bytes 1048608 | tf_op jit(solution)/shard_map/ppermute | solution.py:171
  183.7 10.9 %collective-permute-done.33 = bf16[1024,512]{1,0:T(8,128)(2,1)S(1)} collective-permute-done((bf16[1024,512]{1,0:T(8,128)(2,1)S(1)}, bf16[1024,512]{1,0:T(8,128)(2,1)S(1)}, u32[]{:S(2)}, u32[]{:S(2)}) %collective-permute-start.33) | collective-permute-done | bytes 1048608 | tf_op jit(solution)/shard_map/ppermute | solution.py:171
  195.0 10.9 %collective-permute-done.39 = bf16[1024,512]{1,0:T(8,128)(2,1)S(1)} collective-permute-done((bf16[1024,512]{1,0:T(8,128)(2,1)S(1)}, bf16[1024,512]{1,0:T(8,128)(2,1)S(1)}, u32[]{:S(2)}, u32[]{:S(2)}) %collective-permute-start.39) | collective-permute-done | bytes 1048608 | tf_op jit(solution)/shard_map/ppermute | solution.py:171
  206.1 3.9 %pad_maximum_fusion = f32[4096,512]{1,0:T(8,128)} fusion(f32[1024,512]{1,0:T(8,128)S(1)} %convert_select_fusion, f32[1024,512]{1,0:T(8,128)S(1)} %convert_select_fusion.1, f32[1024,512]{1,0:T(8,128)S(1)} %convert_select_fusion.2, f32[1024,512]{1,0:T(8,128)S(1)} %convert_select_fusion.3), kind=kLoop, calls=%fused_computation | loop fusion | flops 6291456 | bytes 16777216 | tf_op jit(solution)/shard_map/concatenate | solution.py:173
  (152 shorter events, 74.0 us)
Async XLA Ops:
  23.4 23.4 %collective-permute-start.3 = (bf16[96,4096]{1,0:T(8,128)(2,1)S(1)}, bf16[96,4096]{1,0:T(8,128)(2,1)S(1)}, u32[]{:S(2)}, u32[]{:S(2)}) collective-permute-start(bf16[96,4096]{1,0:T(8,128)(2,1)S(1)} %constant_dynamic-update-slice_fusion.refs_0_), channel_id=1, source_target_pairs={{0,2},{2,4},{4,6},{6,0},{8,10},{10,12},{12,14},{14,8},{16,18},{18,... | collective-permute-start | bytes 2359304 | tf_op jit(solution)/shard_map/ppermute | solution.py:29
  23.8 23.9 %collective-permute-start.4 = (bf16[96,4096]{1,0:T(8,128)(2,1)S(1)}, bf16[96,4096]{1,0:T(8,128)(2,1)S(1)}, u32[]{:S(2)}, u32[]{:S(2)}) collective-permute-start(bf16[96,4096]{1,0:T(8,128)(2,1)S(1)} %constant_dynamic-update-slice_fusion.refs_0_), channel_id=1, source_target_pairs={{0,6},{2,0},{4,2},{6,4},{8,14},{10,8},{12,10},{14,12},{16,22},{18,... | collective-permute-start | bytes 2359304 | tf_op jit(solution)/shard_map/ppermute | solution.py:29
  26.1 21.6 %collective-permute-start.5 = (bf16[96,4096]{1,0:T(8,128)(2,1)S(1)}, bf16[96,4096]{1,0:T(8,128)(2,1)S(1)}, u32[]{:S(2)}, u32[]{:S(2)}) collective-permute-start(bf16[96,4096]{1,0:T(8,128)(2,1)S(1)} %constant_dynamic-update-slice_fusion.refs_0_), channel_id=1, source_target_pairs={{0,4},{2,6},{4,0},{6,2},{8,12},{10,14},{12,8},{14,10},{16,20},{18,... | collective-permute-start | bytes 2359304 | tf_op jit(solution)/shard_map/ppermute | solution.py:29
  39.5 17.4 %collective-permute-start.16 = (bf16[384,1024]{1,0:T(8,128)(2,1)S(1)}, bf16[384,1024]{1,0:T(8,128)(2,1)S(1)}, u32[]{:S(2)}, u32[]{:S(2)}) collective-permute-start(bf16[384,1024]{1,0:T(8,128)(2,1)S(1)} %constant_dynamic-update-slice_fusion.4), channel_id=1, source_target_pairs={{0,1},{1,64},{64,65},{65,0},{2,3},{3,66},{66,67},{67,2},{4,5},{5,6... | collective-permute-start | bytes 2359304 | tf_op jit(solution)/shard_map/ppermute | solution.py:18
  40.2 19.4 %collective-permute-start.17 = (bf16[384,1024]{1,0:T(8,128)(2,1)S(1)}, bf16[384,1024]{1,0:T(8,128)(2,1)S(1)}, u32[]{:S(2)}, u32[]{:S(2)}) collective-permute-start(bf16[384,1024]{1,0:T(8,128)(2,1)S(1)} %constant_dynamic-update-slice_fusion.4), channel_id=1, source_target_pairs={{0,65},{1,0},{64,1},{65,64},{2,67},{3,2},{66,3},{67,66},{4,69},{5,... | collective-permute-start | bytes 2359304 | tf_op jit(solution)/shard_map/ppermute | solution.py:18
  53.2 13.6 %collective-permute-start.6 = (bf16[384,1024]{1,0:T(8,128)(2,1)}, bf16[384,1024]{1,0:T(8,128)(2,1)S(1)}, u32[]{:S(2)}, u32[]{:S(2)}) collective-permute-start(bf16[384,1024]{1,0:T(8,128)(2,1)} %get-tuple-element.33.refs_0_), channel_id=1, source_target_pairs={{0,8},{2,10},{4,12},{6,14},{8,16},{10,18},{12,20},{14,22},{16,24},... | collective-permute-start | bytes 2359304 | tf_op jit(solution)/shard_map/ppermute | solution.py:29
  54.9 13.4 %collective-permute-start.7 = (bf16[384,1024]{1,0:T(8,128)(2,1)}, bf16[384,1024]{1,0:T(8,128)(2,1)S(1)}, u32[]{:S(2)}, u32[]{:S(2)}) collective-permute-start(bf16[384,1024]{1,0:T(8,128)(2,1)} %get-tuple-element.33.refs_0_), channel_id=1, source_target_pairs={{0,24},{2,26},{4,28},{6,30},{8,0},{10,2},{12,4},{14,6},{16,8},{18,... | collective-permute-start | bytes 2359304 | tf_op jit(solution)/shard_map/ppermute | solution.py:29
  56.9 18.2 %collective-permute-start.22 = (bf16[384,1024]{1,0:T(8,128)(2,1)}, bf16[384,1024]{1,0:T(8,128)(2,1)S(1)}, u32[]{:S(2)}, u32[]{:S(2)}) collective-permute-start(bf16[384,1024]{1,0:T(8,128)(2,1)} %get-tuple-element.44.refs_0_), channel_id=1, source_target_pairs={{0,8},{2,10},{4,12},{6,14},{8,16},{10,18},{12,20},{14,22},{16,24},... | collective-permute-start | bytes 2359304 | tf_op jit(solution)/shard_map/ppermute | solution.py:29
  56.9 19.1 %collective-permute-start.23 = (bf16[384,1024]{1,0:T(8,128)(2,1)}, bf16[384,1024]{1,0:T(8,128)(2,1)S(1)}, u32[]{:S(2)}, u32[]{:S(2)}) collective-permute-start(bf16[384,1024]{1,0:T(8,128)(2,1)} %get-tuple-element.44.refs_0_), channel_id=1, source_target_pairs={{0,24},{2,26},{4,28},{6,30},{8,0},{10,2},{12,4},{14,6},{16,8},{18,... | collective-permute-start | bytes 2359304 | tf_op jit(solution)/shard_map/ppermute | solution.py:29
  59.6 19.8 %collective-permute-start.18 = (bf16[192,1024]{1,0:T(8,128)(2,1)S(1)}, bf16[192,1024]{1,0:T(8,128)(2,1)S(1)}, u32[]{:S(2)}, u32[]{:S(2)}) collective-permute-start(bf16[192,1024]{1,0:T(8,128)(2,1)S(1)} %slice.42), channel_id=1, source_target_pairs={{0,1},{1,64},{64,65},{65,0},{2,3},{3,66},{66,67},{67,2},{4,5},{5,6... | collective-permute-start | bytes 1179656 | tf_op jit(solution)/shard_map/ppermute | solution.py:18
  75.2 30.4 %collective-permute-start.28 = (bf16[384,1024]{1,0:T(8,128)(2,1)S(1)}, bf16[384,1024]{1,0:T(8,128)(2,1)S(1)}, u32[]{:S(2)}, u32[]{:S(2)}) collective-permute-start(bf16[384,1024]{1,0:T(8,128)(2,1)S(1)} %copy-done.14), channel_id=1, source_target_pairs={{0,8},{2,10},{4,12},{6,14},{8,16},{10,18},{12,20},{14,22},{16,24},... | collective-permute-start | bytes 2359304 | tf_op jit(solution)/shard_map/ppermute | solution.py:29
  76.0 40.5 %collective-permute-start.29 = (bf16[384,1024]{1,0:T(8,128)(2,1)S(1)}, bf16[384,1024]{1,0:T(8,128)(2,1)S(1)}, u32[]{:S(2)}, u32[]{:S(2)}) collective-permute-start(bf16[384,1024]{1,0:T(8,128)(2,1)S(1)} %copy-done.14), channel_id=1, source_target_pairs={{0,24},{2,26},{4,28},{6,30},{8,0},{10,2},{12,4},{14,6},{16,8},{18,... | collective-permute-start | bytes 2359304 | tf_op jit(solution)/shard_map/ppermute | solution.py:29
  79.7 26.4 %collective-permute-start.24 = (bf16[192,1024]{1,0:T(8,128)(2,1)}, bf16[192,1024]{1,0:T(8,128)(2,1)S(1)}, u32[]{:S(2)}, u32[]{:S(2)}) collective-permute-start(bf16[192,1024]{1,0:T(8,128)(2,1)} %slice.44), channel_id=1, source_target_pairs={{0,8},{2,10},{4,12},{6,14},{8,16},{10,18},{12,20},{14,22},{16,24},... | collective-permute-start | bytes 1179656 | tf_op jit(solution)/shard_map/ppermute | solution.py:29
  81.6 24.5 %collective-permute-start.25 = (bf16[192,1024]{1,0:T(8,128)(2,1)}, bf16[192,1024]{1,0:T(8,128)(2,1)}, u32[]{:S(2)}, u32[]{:S(2)}) collective-permute-start(bf16[192,1024]{1,0:T(8,128)(2,1)} %slice.45), channel_id=1, source_target_pairs={{0,24},{2,26},{4,28},{6,30},{8,0},{10,2},{12,4},{14,6},{16,8},{18,... | collective-permute-start | bytes 1179656 | tf_op jit(solution)/shard_map/ppermute | solution.py:29
  100.4 53.2 %collective-permute-start.20 = (f32[1024,512]{1,0:T(8,128)}, f32[1024,512]{1,0:T(8,128)}, u32[]{:S(2)}, u32[]{:S(2)}) collective-permute-start(f32[1024,512]{1,0:T(8,128)} %get-tuple-element.43), channel_id=1, source_target_pairs={{0,32},{32,0},{1,33},{33,1},{2,34},{34,2},{3,35},{35,3},{4,36},{36... | collective-permute-start | bytes 6291464 | tf_op jit(solution)/shard_map/ppermute | solution.py:170
  106.1 28.7 %collective-permute-start.34 = (bf16[384,1024]{1,0:T(8,128)(2,1)S(1)}, bf16[384,1024]{1,0:T(8,128)(2,1)S(1)}, u32[]{:S(2)}, u32[]{:S(2)}) collective-permute-start(bf16[384,1024]{1,0:T(8,128)(2,1)S(1)} %copy-done.13), channel_id=1, source_target_pairs={{0,8},{2,10},{4,12},{6,14},{8,16},{10,18},{12,20},{14,22},{16,24},... | collective-permute-start | bytes 2359304 | tf_op jit(solution)/shard_map/ppermute | solution.py:29
  106.2 28.7 %collective-permute-start.35 = (bf16[384,1024]{1,0:T(8,128)(2,1)S(1)}, bf16[384,1024]{1,0:T(8,128)(2,1)S(1)}, u32[]{:S(2)}, u32[]{:S(2)}) collective-permute-start(bf16[384,1024]{1,0:T(8,128)(2,1)S(1)} %copy-done.13), channel_id=1, source_target_pairs={{0,24},{2,26},{4,28},{6,30},{8,0},{10,2},{12,4},{14,6},{16,8},{18,... | collective-permute-start | bytes 2359304 | tf_op jit(solution)/shard_map/ppermute | solution.py:29
  116.6 42.1 %collective-permute-start.26 = (f32[1024,512]{1,0:T(8,128)}, f32[1024,512]{1,0:T(8,128)}, u32[]{:S(2)}, u32[]{:S(2)}) collective-permute-start(f32[1024,512]{1,0:T(8,128)} %get-tuple-element.46), channel_id=1, source_target_pairs={{0,32},{32,0},{1,33},{33,1},{2,34},{34,2},{3,35},{35,3},{4,36},{36... | collective-permute-start | bytes 6291464 | tf_op jit(solution)/shard_map/ppermute | solution.py:170
  133.0 30.9 %collective-permute-start.32 = (f32[1024,512]{1,0:T(8,128)}, f32[1024,512]{1,0:T(8,128)}, u32[]{:S(2)}, u32[]{:S(2)}) collective-permute-start(f32[1024,512]{1,0:T(8,128)} %get-tuple-element.49), channel_id=1, source_target_pairs={{0,32},{32,0},{1,33},{33,1},{2,34},{34,2},{3,35},{35,3},{4,36},{36... | collective-permute-start | bytes 6291464 | tf_op jit(solution)/shard_map/ppermute | solution.py:170
  152.3 16.6 %collective-permute-start.38 = (f32[1024,512]{1,0:T(8,128)}, f32[1024,512]{1,0:T(8,128)}, u32[]{:S(2)}, u32[]{:S(2)}) collective-permute-start(f32[1024,512]{1,0:T(8,128)} %get-tuple-element.52), channel_id=1, source_target_pairs={{0,32},{32,0},{1,33},{33,1},{2,34},{34,2},{3,35},{35,3},{4,36},{36... | collective-permute-start | bytes 6291464 | tf_op jit(solution)/shard_map/ppermute | solution.py:170
  156.0 17.9 %collective-permute-start.21 = (bf16[1024,512]{1,0:T(8,128)(2,1)S(1)}, bf16[1024,512]{1,0:T(8,128)(2,1)S(1)}, u32[]{:S(2)}, u32[]{:S(2)}) collective-permute-start(bf16[1024,512]{1,0:T(8,128)(2,1)S(1)} %get-tuple-element.53), channel_id=1, source_target_pairs={{1,32},{32,1},{3,34},{34,3},{5,36},{36,5},{7,38},{38,7},{9,40},{40... | collective-permute-start | bytes 3145736 | tf_op jit(solution)/shard_map/ppermute | solution.py:171
  161.0 22.3 %collective-permute-start.27 = (bf16[1024,512]{1,0:T(8,128)(2,1)S(1)}, bf16[1024,512]{1,0:T(8,128)(2,1)S(1)}, u32[]{:S(2)}, u32[]{:S(2)}) collective-permute-start(bf16[1024,512]{1,0:T(8,128)(2,1)S(1)} %get-tuple-element.55), channel_id=1, source_target_pairs={{1,32},{32,1},{3,34},{34,3},{5,36},{36,5},{7,38},{38,7},{9,40},{40... | collective-permute-start | bytes 3145736 | tf_op jit(solution)/shard_map/ppermute | solution.py:171
  166.2 28.4 %collective-permute-start.33 = (bf16[1024,512]{1,0:T(8,128)(2,1)S(1)}, bf16[1024,512]{1,0:T(8,128)(2,1)S(1)}, u32[]{:S(2)}, u32[]{:S(2)}) collective-permute-start(bf16[1024,512]{1,0:T(8,128)(2,1)S(1)} %get-tuple-element.57), channel_id=1, source_target_pairs={{1,32},{32,1},{3,34},{34,3},{5,36},{36,5},{7,38},{38,7},{9,40},{40... | collective-permute-start | bytes 3145736 | tf_op jit(solution)/shard_map/ppermute | solution.py:171
  171.0 34.8 %collective-permute-start.39 = (bf16[1024,512]{1,0:T(8,128)(2,1)S(1)}, bf16[1024,512]{1,0:T(8,128)(2,1)S(1)}, u32[]{:S(2)}, u32[]{:S(2)}) collective-permute-start(bf16[1024,512]{1,0:T(8,128)(2,1)S(1)} %get-tuple-element.59), channel_id=1, source_target_pairs={{1,32},{32,1},{3,34},{34,3},{5,36},{36,5},{7,38},{38,7},{9,40},{40... | collective-permute-start | bytes 3145736 | tf_op jit(solution)/shard_map/ppermute | solution.py:171
  (44 other events, 359.3 us)

commit v2 on v1

--- a/solution.py
+++ b/solution.py
@@ -10,8 +10,8 @@
 
 NAMES = ("zh", "c", "y", "x", "zl")
 SIZES = (2, 2, 4, 4, 2)
-CHUNKS = 4
-VMEM = 56 * 1024 * 1024
+CHUNKS = (4, 6, 4, 2)
+SCOPED = 8 * 1024 * 1024
 
 
 def z_shift(value, step):
@@ -29,21 +29,16 @@
     return lax.ppermute(value, ("c", "y", "x"), table)
 
 
-def whole(shape):
-    return pl.BlockSpec(shape, lambda: (0,) * len(shape))
-
-
 def in_vmem(kernel, outs, *args):
     return pl.pallas_call(
         kernel,
         out_shape=outs,
         in_specs=[
-            pl.BlockSpec(memory_space=pltpu.SMEM)
-            if a.dtype == jnp.int32 else whole(a.shape)
-            for a in args
+            pl.BlockSpec(memory_space=pltpu.SMEM if v.dtype == jnp.int32 else pltpu.VMEM)
+            for v in args
         ],
-        out_specs=jax.tree.map(lambda o: whole(o.shape), outs),
-        compiler_params=pltpu.CompilerParams(vmem_limit_bytes=VMEM),
+        out_specs=[pl.BlockSpec(memory_space=pltpu.VMEM)] * len(outs),
+        compiler_params=pltpu.CompilerParams(vmem_limit_bytes=SCOPED),
     )(*args)
 
 
@@ -112,22 +107,46 @@
     block = min(256, width)
 
     def kernel(*refs):
-        rows = jnp.concatenate([r[...] for r in refs[: len(pieces)]], axis=0)
-        total = lax.dot_general(
-            rows, refs[len(pieces)][...], (((0,), (0,)), ((), ())), preferred_element_type=jnp.float32
-        )
-        refs[-2][...] = total[:, :half]
-        refs[-1][...] = total[:, half:]
-
+        mine, other = refs[-2:]
+        right = refs[len(pieces)][...]
+        for at in range(0, width, block):
+            left = jnp.concatenate([r[:, at : at + block] for r in refs[: len(pieces)]], axis=0)
+            total = lax.dot_general(
+                left, right, (((0,), (0,)), ((), ())), preferred_element_type=jnp.float32
+            )
+            mine[at : at + block, :] = total[:, :half]
+            other[at : at + block, :] = total[:, half:].astype(jnp.bfloat16)
+
+    outs = [shape_of(width, half, jnp.float32), shape_of(width, half)]
+    return in_vmem(kernel, outs, *pieces, columns)
+
+
+def core_swap(value):
+    return lax.ppermute(value, "c", [(0, 1), (1, 0)])
+
+
+def write_out(out, total, at, stays, mine, moved):
+    width, cols = mine.shape
+
+    def kernel(stays_ref, mine_ref, moved_ref, *refs):
+        out_ref, buffer, sem = refs[-3:]
+        buffer[...] = jnp.where(stays_ref[0] == 1, mine_ref[...], moved_ref[...].astype(jnp.float32))
+        copy = pltpu.make_async_copy(buffer, out_ref.at[pl.ds(at, width), :], sem)
+        copy.start()
+        copy.wait()
+
+    args = [stays, mine, moved] + ([] if out is None else [out])
     return pl.pallas_call(
         kernel,
-        grid=(width // block,),
-        in_specs=[pl.BlockSpec((p.shape[0], block), lambda i: (0, i)) for p in pieces]
-        + [pl.BlockSpec(columns.shape, lambda i: (0, 0))],
-        out_specs=[pl.BlockSpec((block, half), lambda i: (i, 0))] * 2,
-        out_shape=[shape_of(width, half, jnp.float32)] * 2,
-        compiler_params=pltpu.CompilerParams(vmem_limit_bytes=VMEM),
-    )(*pieces, columns)
+        out_shape=shape_of(total, cols, jnp.float32),
+        in_specs=[pl.BlockSpec(memory_space=pltpu.SMEM)]
+        + [pl.BlockSpec(memory_space=pltpu.VMEM)] * 2
+        + ([] if out is None else [pl.BlockSpec(memory_space=pl.ANY)]),
+        out_specs=pl.BlockSpec(memory_space=pl.ANY),
+        scratch_shapes=[pltpu.VMEM((width, cols), jnp.float32), pltpu.SemaphoreType.DMA(())],
+        input_output_aliases={} if out is None else {3: 0},
+        compiler_params=pltpu.CompilerParams(vmem_limit_bytes=SCOPED),
+    )(*args)
 
 
 def on_device(jacobian, obs_weights, time_to_obs):
@@ -144,33 +163,71 @@
     )
     cut = split_rows(place, jacobian, jnp.sqrt(picked)[:, None])
 
-    first = [cut[4]] + [ring_shift(cut[4 + n], s, 0) for n, s in ((1, 1), (2, -1), (3, 2))]
-    groups = regroup_columns(place, first)
-    second = [groups[0]] + [ring_shift(groups[n], s, 1) for n, s in ((1, 1), (2, -1), (3, 2))]
-    flat = jnp.concatenate(second, axis=0)
-    back = z_shift(flat, 1)
-    front = z_shift(flat, -1)
+    with jax.named_scope("columns_first"):
+        first = [cut[4]] + [ring_shift(cut[4 + n], s, 0) for n, s in ((1, 1), (2, -1), (3, 2))]
+        groups = regroup_columns(place, first)
+    with jax.named_scope("columns_second"):
+        second = [groups[0]] + [ring_shift(groups[n], s, 1) for n, s in ((1, 1), (2, -1), (3, 2))]
+        flat = jnp.concatenate(second, axis=0)
+    with jax.named_scope("columns_near"):
+        back = z_shift(flat, 1)
+        front = z_shift(flat, -1)
+        columns_near = [back, front]
     mid = flat.shape[0] // 2
-    far = [z_shift(back[:mid], 1), z_shift(front[mid:], -1)]
-    columns = jnp.stack([flat, back, front, jnp.concatenate(far, axis=0)])
-    columns = columns.reshape(4, 16, rows, wide).transpose(1, 0, 2, 3).reshape(64 * rows, wide)
-
-    column = jnp.concatenate(
-        [cut[0]] + [z_shift(cut[n], s) for n, s in ((1, 1), (2, -1), (3, 2))], axis=0
-    )
-    ring = [column] + [ring_shift(column, s, 0) for s in (1, -1, 2)]
-    widths = [quarter // CHUNKS] * CHUNKS
-    done = []
-    for group in stack_chunks(ring, widths):
-        back = ring_shift(group, 1, 1)
-        front = ring_shift(group, -1, 1)
+    with jax.named_scope("columns_far"):
+        far = columns_far = [z_shift(back[:mid], 1), z_shift(front[mid:], -1)]
+        columns = jnp.stack([flat, back, front, jnp.concatenate(far, axis=0)])
+        columns = columns.reshape(4, 16, rows, wide).transpose(1, 0, 2, 3).reshape(64 * rows, wide)
+
+    with jax.named_scope("panel_z"):
+        column = jnp.concatenate(
+            [cut[0]] + [z_shift(cut[n], s) for n, s in ((1, 1), (2, -1), (3, 2))], axis=0
+        )
+        column, _ = lax.optimization_barrier((column, flat))
+    with jax.named_scope("panel_ring"):
+        ring = [column] + [ring_shift(column, s, 0) for s in (1, -1, 2)]
+    widths = [quarter // 16 * n for n in CHUNKS]
+    near, far = [], []
+    ring, _ = lax.optimization_barrier((ring, columns_near))
+    for n, group in enumerate(stack_chunks(ring, widths)):
+        if n > 1:
+            group, _ = lax.optimization_barrier((group, far[n - 2]))
+        with jax.named_scope(f"near{n}"):
+            back = ring_shift(group, 1, 1)
+            front = ring_shift(group, -1, 1)
         mid = group.shape[0] // 2
-        far = [ring_shift(back[:mid], 1, 1), ring_shift(front[mid:], -1, 1)]
-        mine, other = products([group, back, front] + far, columns)
-        mine = mine + lax.ppermute(other, "c", [(0, 1), (1, 0)])
-        moved = lax.ppermute(mine.astype(jnp.bfloat16), ("c", "zl"), [(1, 2), (2, 1)])
-        done.append(jnp.where(c == zl, mine, moved.astype(jnp.float32)))
-    return jnp.concatenate(done, axis=0)
+        near.append([group, back, front])
+        before = far[n - 1] if n > 0 else columns_far
+        (back, front), _ = lax.optimization_barrier(((back, front), before))
+        with jax.named_scope(f"far{n}"):
+            far.append([ring_shift(back[:mid], 1, 1), ring_shift(front[mid:], -1, 1)])
+    sums, sent, last = [], [], len(widths) - 1
+    for n in range(len(widths)):
+        with jax.named_scope(f"product{n}"):
+            mine, other = products(near[n] + far[n], columns)
+        gate = []
+        if n == 0:
+            gate += near[1][1:]
+        elif n < last:
+            gate += far[n + 1]
+        if 0 < n and n + 1 < last:
+            gate += near[n + 2][1:]
+        if n > 0:
+            gate.append(sent[n - 1])
+            gate.append(sums[max(n - 2, 0)][1])
+        other, _ = lax.optimization_barrier((other, gate))
+        with jax.named_scope(f"exchange{n}"):
+            mine = mine + core_swap(other).astype(jnp.float32)
+            sent.append(mine.astype(jnp.bfloat16))
+        with jax.named_scope(f"swap{n}"):
+            sums.append((mine, lax.ppermute(sent[n], ("c", "zl"), [(1, 2), (2, 1)])))
+    stays = (c == zl).astype(jnp.int32).reshape(1)
+    stays, _ = lax.optimization_barrier((stays, sent))
+    out, at = None, 0
+    for width, (mine, moved) in zip(widths, sums):
+        out = write_out(out, quarter, at, stays, mine, moved)
+        at += width
+    return out
 
 
 def solution(mesh):

time: 211 us -> 174 us (0.82)
  Pallas kernels: 39.3 us -> 24 us
  other arithmetic: 17.9 us -> 7.28 us
  starting transfers between devices: 63.6 us -> 58.5 us
  local copies, waits for them, and re-layouts: 10.9 us -> 7.2 us
  waiting for transfers between devices: 78 us -> 75.5 us
    pallas_call x4, Pallas kernels: 31 us -> 8.51 us  [write_out(): pl.pallas_call(kernel, out_shape=shape_of(total, cols, jnp.float32), in_s...]
    ppermute x7, waiting for transfers between devices: 3.11 us -> 20.4 us  [z_shift(): lax.ppermute(value, ('zh', 'zl'), [(z, (z + step) % 4) for z in range(4)])]
    ppermute x8, waiting for transfers between devices: 30.8 us -> 19.1 us  [the longest x4 16.5 us: on_device(): sums.append((mine, lax.ppermute(sent[n], ('c', 'zl'), [(1, 2), (2, 1)])))]
    ppermute x25, waiting for transfers between devices: 44.1 us -> 36 us  [ring_shift(): return lax.ppermute(value, ('c', 'y', 'x'), table)]
    pallas_call x3 -> x7, Pallas kernels: 8.27 us -> 15.5 us  [in_vmem(): pl.pallas_call(kernel, out_shape=outs, in_specs=[pl.BlockSpec(memory_spac...]
    ppermute x8, starting transfers between devices: 20.3 us -> 15.8 us  [the longest x4 9.59 us: on_device(): sums.append((mine, lax.ppermute(sent[n], ('c', 'zl'), [(1, 2), (2, 1)])))]
    concatenate x1, other arithmetic: 3.92 us -> 0.05 us  [on_device(): jnp.concatenate([cut[0]] + [z_shift(cut[n], s) for n, s in ((1, 1), (2, -...]
    convert_element_type x4, other arithmetic: 9.03 us -> 5.75 us  [on_device(): sent.append(mine.astype(jnp.bfloat16))]
  transfers between devices with their start and end apart: 40 -> 40, of which waited for: 13 -> 20; matrix products, arithmetic and copies ran while one was open for 8% -> 4% of each run, Pallas kernels for 18% -> 12%
where the time goes in v2:
time: 174 us; the launch traced here: 173 us
  waiting for transfers between devices  75.5 us (43%)
  starting transfers between devices  58.5 us (34%)
  Pallas kernels  24 us (14%)
  other arithmetic  7.28 us (4%)
  local copies, waits for them, and re-layouts  7.2 us (4%)
    ppermute x25, waiting for transfers between devices, ring_shift(): return lax.ppermute(value, ('c', 'y', 'x'), table)  36 us
    ppermute x25, starting transfers between devices, ring_shift(): return lax.ppermute(value, ('c', 'y', 'x'), table)  30.4 us
    ppermute x7, waiting for transfers between devices, z_shift(): lax.ppermute(value, ('zh', 'zl'), [(z, (z + step) % 4) for z in range(4)])  20.4 us
    ppermute x4, waiting for transfers between devices, on_device(): sums.append((mine, lax.ppermute(sent[n], ('c', 'zl'), [(1, 2), (2, 1)])))  16.5 us
    pallas_call x7, Pallas kernels, in_vmem(): pl.pallas_call(kernel, out_shape=outs, in_specs=[pl.BlockSpec(memory_spac...  15.5 us
    ppermute x7, starting transfers between devices, z_shift(): lax.ppermute(value, ('zh', 'zl'), [(z, (z + step) % 4) for z in range(4)])  12.4 us
    ppermute x4, starting transfers between devices, on_device(): sums.append((mine, lax.ppermute(sent[n], ('c', 'zl'), [(1, 2), (2, 1)])))  9.59 us
    pallas_call x4, Pallas kernels, write_out(): pl.pallas_call(kernel, out_shape=shape_of(total, cols, jnp.float32), in_s...  8.51 us
  transfers between devices with their start and end apart: 40, of which 20 were waited for; matrix products, arithmetic and copies ran while one was open for 4% of the time, Pallas kernels for 12%

profile of v2, /device:TPU:1, one launch (start us, length us, event | category | flops | bytes accessed | tf_op | source)
XLA Modules:
  0.0 173.1 jit_solution(3614024758943162350)
XLA Ops:
  3.1 2.2 %collective-permute-start.3 = (bf16[24,4096]{1,0:T(8,128)(2,1)S(1)}, bf16[24,4096]{1,0:T(8,128)(2,1)S(1)}, u32[]{:S(2)}, u32[]{:S(2)}) collective-permute-start(bf16[24,4096]{1,0:T(8,128)(2,1)S(1)} %get-tuple-element.54), channel_id=1, source_target_pairs={{0,2},{2,4},{4,6},{6,0},{8,10},{10,12},{12,14},{14,8},{16,18},{18,... | collective-permute-start | bytes 589832 | tf_op jit(solution)/shard_map/columns_first/ppermute | solution.py:29
  17.1 3.1 %collective-permute-start.8 = (bf16[96,1024]{1,0:T(8,128)(2,1)S(1)}, bf16[96,1024]{1,0:T(8,128)(2,1)S(1)}, u32[]{:S(2)}, u32[]{:S(2)}) collective-permute-start(bf16[96,1024]{1,0:T(8,128)(2,1)S(1)} %get-tuple-element.60), channel_id=1, source_target_pairs={{0,16},{2,18},{4,20},{6,22},{8,24},{10,26},{12,28},{14,30},{16,0},... | collective-permute-start | bytes 589832 | tf_op jit(solution)/shard_map/columns_second/ppermute | solution.py:29
  23.2 3.5 %collective-permute-start.13 = (bf16[384,1024]{1,0:T(8,128)(2,1)S(1)}, bf16[384,1024]{1,0:T(8,128)(2,1)S(1)}, u32[]{:S(2)}, u32[]{:S(2)}) collective-permute-start(bf16[384,1024]{1,0:T(8,128)(2,1)S(1)} %constant_dynamic-update-slice_fusion), channel_id=1, source_target_pairs={{0,65},{1,0},{64,1},{65,64},{2,67},{3,2},{66,3},{67,66},{4,69},{5,... | collective-permute-start | bytes 2359304 | tf_op jit(solution)/shard_map/columns_near/ppermute | solution.py:18
  30.0 10.3 %collective-permute-done.13 = bf16[384,1024]{1,0:T(8,128)(2,1)S(1)} collective-permute-done((bf16[384,1024]{1,0:T(8,128)(2,1)S(1)}, bf16[384,1024]{1,0:T(8,128)(2,1)S(1)}, u32[]{:S(2)}, u32[]{:S(2)}) %collective-permute-start.13) | collective-permute-done | bytes 786464 | tf_op jit(solution)/shard_map/columns_near/ppermute | solution.py:18
  40.3 3.5 %collective-permute-start.17 = (bf16[192,1024]{1,0:T(8,128)(2,1)S(1)}, bf16[192,1024]{1,0:T(8,128)(2,1)S(1)}, u32[]{:S(2)}, u32[]{:S(2)}) collective-permute-start(bf16[192,1024]{1,0:T(8,128)(2,1)S(1)} %slice.41), channel_id=1, source_target_pairs={{0,65},{1,0},{64,1},{65,64},{2,67},{3,2},{66,3},{67,66},{4,69},{5,... | collective-permute-start | bytes 1179656 | tf_op jit(solution)/shard_map/columns_far/ppermute | solution.py:18
  43.8 3.3 %collective-permute-done.10.refs_2_ = bf16[96,4096]{1,0:T(8,128)(2,1)S(1)} collective-permute-done((bf16[96,4096]{1,0:T(8,128)(2,1)S(1)}, bf16[96,4096]{1,0:T(8,128)(2,1)S(1)}, u32[]{:S(2)}, u32[]{:S(2)}) %collective-permute-start.10) | collective-permute-done | bytes 786464 | tf_op jit(solution)/shard_map/panel_ring/ppermute | solution.py:29
  49.8 2.7 %collective-permute-start.21 = (bf16[384,1536]{1,0:T(8,128)(2,1)S(1)}, bf16[384,1536]{1,0:T(8,128)(2,1)S(1)}, u32[]{:S(2)}, u32[]{:S(2)}) collective-permute-start(bf16[384,1536]{1,0:T(8,128)(2,1)S(1)} %get-tuple-element.71.refs_0_), channel_id=1, source_target_pairs={{0,24},{2,26},{4,28},{6,30},{8,0},{10,2},{12,4},{14,6},{16,8},{18,... | collective-permute-start | bytes 3538952 | tf_op jit(solution)/shard_map/near1/ppermute | solution.py:29
  52.6 9.1 %collective-permute-done.16 = bf16[192,1024]{1,0:T(8,128)(2,1)S(1)} collective-permute-done((bf16[192,1024]{1,0:T(8,128)(2,1)S(1)}, bf16[192,1024]{1,0:T(8,128)(2,1)S(1)}, u32[]{:S(2)}, u32[]{:S(2)}) %collective-permute-start.16) | collective-permute-done | bytes 393248 | tf_op jit(solution)/shard_map/columns_far/ppermute | solution.py:18
  62.2 2.8 %collective-permute-start.19 = (bf16[192,1024]{1,0:T(8,128)(2,1)S(1)}, bf16[192,1024]{1,0:T(8,128)(2,1)S(1)}, u32[]{:S(2)}, u32[]{:S(2)}) collective-permute-start(bf16[192,1024]{1,0:T(8,128)(2,1)S(1)} %slice.33), channel_id=1, source_target_pairs={{0,24},{2,26},{4,28},{6,30},{8,0},{10,2},{12,4},{14,6},{16,8},{18,... | collective-permute-start | bytes 1179656 | tf_op jit(solution)/shard_map/far0/ppermute | solution.py:29
  65.5 10.8 %collective-permute-done.19.refs_4_ = bf16[192,1024]{1,0:T(8,128)(2,1)S(1)} collective-permute-done((bf16[192,1024]{1,0:T(8,128)(2,1)S(1)}, bf16[192,1024]{1,0:T(8,128)(2,1)S(1)}, u32[]{:S(2)}, u32[]{:S(2)}) %collective-permute-start.19) | collective-permute-done | bytes 393248 | tf_op jit(solution)/shard_map/far0/ppermute | solution.py:29
  76.3 2.7 %collective-permute-done.18.refs_3_ = bf16[192,1024]{1,0:T(8,128)(2,1)S(1)} collective-permute-done((bf16[192,1024]{1,0:T(8,128)(2,1)S(1)}, bf16[192,1024]{1,0:T(8,128)(2,1)S(1)}, u32[]{:S(2)}, u32[]{:S(2)}) %collective-permute-start.18) | collective-permute-done | bytes 393248 | tf_op jit(solution)/shard_map/far0/ppermute | solution.py:29
  79.0 3.5 %product0.1 = (f32[1024,512]{1,0:T(8,128)S(1)}, bf16[1024,512]{1,0:T(8,128)(2,1)S(1)}) custom-call(bf16[384,1024]{1,0:T(8,128)(2,1)S(1)} %get-tuple-element.66.refs_0_, bf16[384,1024]{1,0:T(8,128)(2,1)S(1)} %collective-permute-done.14.refs_1_, bf16[384,1024]{1,0:T(8,128)(2,1)S(1)} %collective-permute-done.15.refs_2_, ...), custom_call_target="tpu_custom_call" | custom-call | tf_op jit(solution)/shard_map/product0/pallas_call | solution.py:33
  82.5 5.7 %collective-permute-start.22 = (bf16[1024,512]{1,0:T(8,128)(2,1)S(1)}, bf16[1024,512]{1,0:T(8,128)(2,1)S(1)}, u32[]{:S(2)}, u32[]{:S(2)}) collective-permute-start(bf16[1024,512]{1,0:T(8,128)(2,1)S(1)} %get-tuple-element.72), channel_id=1, source_target_pairs={{0,32},{32,0},{1,33},{33,1},{2,34},{34,2},{3,35},{35,3},{4,36},{36... | collective-permute-start | bytes 3145736 | tf_op jit(solution)/shard_map/exchange0/ppermute | solution.py:125
  94.2 2.2 %collective-permute-start.24 = (bf16[192,1536]{1,0:T(8,128)(2,1)S(1)}, bf16[192,1536]{1,0:T(8,128)(2,1)S(1)}, u32[]{:S(2)}, u32[]{:S(2)}) collective-permute-start(bf16[192,1536]{1,0:T(8,128)(2,1)S(1)} %slice.35), channel_id=1, source_target_pairs={{0,24},{2,26},{4,28},{6,30},{8,0},{10,2},{12,4},{14,6},{16,8},{18,... | collective-permute-start | bytes 1769480 | tf_op jit(solution)/shard_map/far1/ppermute | solution.py:29
  96.4 9.3 %collective-permute-done.24.refs_4_ = bf16[192,1536]{1,0:T(8,128)(2,1)S(1)} collective-permute-done((bf16[192,1536]{1,0:T(8,128)(2,1)S(1)}, bf16[192,1536]{1,0:T(8,128)(2,1)S(1)}, u32[]{:S(2)}, u32[]{:S(2)}) %collective-permute-start.24) | collective-permute-done | bytes 589856 | tf_op jit(solution)/shard_map/far1/ppermute | solution.py:29
  105.7 2.6 %collective-permute-done.23.refs_3_ = bf16[192,1536]{1,0:T(8,128)(2,1)S(1)} collective-permute-done((bf16[192,1536]{1,0:T(8,128)(2,1)S(1)}, bf16[192,1536]{1,0:T(8,128)(2,1)S(1)}, u32[]{:S(2)}, u32[]{:S(2)}) %collective-permute-start.23) | collective-permute-done | bytes 589856 | tf_op jit(solution)/shard_map/far1/ppermute | solution.py:29
  111.4 5.1 %product1.1 = (f32[1536,512]{1,0:T(8,128)S(1)}, bf16[1536,512]{1,0:T(8,128)(2,1)S(1)}) custom-call(bf16[384,1536]{1,0:T(8,128)(2,1)S(1)} %get-tuple-element.71.refs_0_, bf16[384,1536]{1,0:T(8,128)(2,1)S(1)} %collective-permute-done.20.refs_1_, bf16[384,1536]{1,0:T(8,128)(2,1)S(1)} %collective-permute-done.21.refs_2_, ...), custom_call_target="tpu_custom_call" | custom-call | tf_op jit(solution)/shard_map/product1/pallas_call | solution.py:33
  116.7 2.7 %collective-permute-done.28.refs_4_ = bf16[192,1024]{1,0:T(8,128)(2,1)S(1)} collective-permute-done((bf16[192,1024]{1,0:T(8,128)(2,1)S(1)}, bf16[192,1024]{1,0:T(8,128)(2,1)S(1)}, u32[]{:S(2)}, u32[]{:S(2)}) %collective-permute-start.28) | collective-permute-done | bytes 393248 | tf_op jit(solution)/shard_map/far2/ppermute | solution.py:29
  127.9 3.5 %product2.1 = (f32[1024,512]{1,0:T(8,128)S(1)}, bf16[1024,512]{1,0:T(8,128)(2,1)S(1)}) custom-call(bf16[384,1024]{1,0:T(8,128)(2,1)S(1)} %get-tuple-element.78.refs_0_, bf16[384,1024]{1,0:T(8,128)(2,1)S(1)} %collective-permute-done.25.refs_1_, bf16[384,1024]{1,0:T(8,128)(2,1)S(1)} %collective-permute-done.26.refs_2_, ...), custom_call_target="tpu_custom_call" | custom-call | tf_op jit(solution)/shard_map/product2/pallas_call | solution.py:33
  136.2 11.3 %collective-permute-done.36.moved_ref = bf16[1536,512]{1,0:T(8,128)(2,1)S(1)} collective-permute-done((bf16[1536,512]{1,0:T(8,128)(2,1)S(1)}, bf16[1536,512]{1,0:T(8,128)(2,1)S(1)}, u32[]{:S(2)}, u32[]{:S(2)}) %collective-permute-start.36) | collective-permute-done | bytes 1572896 | tf_op jit(solution)/shard_map/swap1/ppermute | solution.py:223
  152.0 3.6 %collective-permute-start.38 = (bf16[512,512]{1,0:T(8,128)(2,1)}, bf16[512,512]{1,0:T(8,128)(2,1)}, u32[]{:S(2)}, u32[]{:S(2)}) collective-permute-start(bf16[512,512]{1,0:T(8,128)(2,1)} %get-tuple-element.93), channel_id=1, source_target_pairs={{1,32},{32,1},{3,34},{34,3},{5,36},{36,5},{7,38},{38,7},{9,40},{40... | collective-permute-start | bytes 1572872 | tf_op jit(solution)/shard_map/swap3/ppermute | solution.py:223
  162.6 2.5 %collective-permute-done.39.moved_ref = bf16[1024,512]{1,0:T(8,128)(2,1)} collective-permute-done((bf16[1024,512]{1,0:T(8,128)(2,1)}, bf16[1024,512]{1,0:T(8,128)(2,1)}, u32[]{:S(2)}, u32[]{:S(2)}) %collective-permute-start.39) | collective-permute-done | bytes 1048608 | tf_op jit(solution)/shard_map/swap2/ppermute | solution.py:223
  165.1 2.9 %shard_map.41.refs_0_ = f32[4096,512]{1,0:T(8,128)} custom-call(s32[1]{0:T(128)} %bitcast.stays_ref, f32[1024,512]{1,0:T(8,128)S(1)} %copy-done.1, bf16[1024,512]{1,0:T(8,128)(2,1)} %collective-permute-done.39.moved_ref, f32[4096,512]{1,0:T(8,128)} %shard_map.40.refs_0_), custom_call_target="tpu_custom_call", output_to_operand_aliasing={{}: (3, {})} | custom-call | tf_op jit(solution)/shard_map/pallas_call | solution.py:139
  168.0 2.7 %collective-permute-done.38.moved_ref = bf16[512,512]{1,0:T(8,128)(2,1)} collective-permute-done((bf16[512,512]{1,0:T(8,128)(2,1)}, bf16[512,512]{1,0:T(8,128)(2,1)}, u32[]{:S(2)}, u32[]{:S(2)}) %collective-permute-start.38) | collective-permute-done | bytes 524320 | tf_op jit(solution)/shard_map/swap3/ppermute | solution.py:223
  (108 shorter events, 61.2 us)
Async XLA Ops:
  10.1 10.1 %collective-permute-start.1 = (bf16[24,4096]{1,0:T(8,128)(2,1)S(1)}, bf16[24,4096]{1,0:T(8,128)(2,1)S(1)}, u32[]{:S(2)}, u32[]{:S(2)}) collective-permute-start(bf16[24,4096]{1,0:T(8,128)(2,1)S(1)} %get-tuple-element.51), channel_id=1, source_target_pairs={{0,65},{1,0},{64,1},{65,64},{2,67},{3,2},{66,3},{67,66},{4,69},{5,... | collective-permute-start | bytes 589832 | tf_op jit(solution)/shard_map/panel_z/ppermute | solution.py:18
  23.2 17.0 %collective-permute-start.13 = (bf16[384,1024]{1,0:T(8,128)(2,1)S(1)}, bf16[384,1024]{1,0:T(8,128)(2,1)S(1)}, u32[]{:S(2)}, u32[]{:S(2)}) collective-permute-start(bf16[384,1024]{1,0:T(8,128)(2,1)S(1)} %constant_dynamic-update-slice_fusion), channel_id=1, source_target_pairs={{0,65},{1,0},{64,1},{65,64},{2,67},{3,2},{66,3},{67,66},{4,69},{5,... | collective-permute-start | bytes 2359304 | tf_op jit(solution)/shard_map/columns_near/ppermute | solution.py:18
  26.8 17.0 %collective-permute-start.11 = (bf16[96,4096]{1,0:T(8,128)(2,1)S(1)}, bf16[96,4096]{1,0:T(8,128)(2,1)S(1)}, u32[]{:S(2)}, u32[]{:S(2)}) collective-permute-start(bf16[96,4096]{1,0:T(8,128)(2,1)S(1)} %pad_maximum_fusion.1.refs_0_), channel_id=1, source_target_pairs={{0,4},{2,6},{4,0},{6,2},{8,12},{10,14},{12,8},{14,10},{16,20},{18,... | collective-permute-start | bytes 2359304 | tf_op jit(solution)/shard_map/panel_ring/ppermute | solution.py:29
  28.1 19.0 %collective-permute-start.10 = (bf16[96,4096]{1,0:T(8,128)(2,1)S(1)}, bf16[96,4096]{1,0:T(8,128)(2,1)S(1)}, u32[]{:S(2)}, u32[]{:S(2)}) collective-permute-start(bf16[96,4096]{1,0:T(8,128)(2,1)S(1)} %pad_maximum_fusion.1.refs_0_), channel_id=1, source_target_pairs={{0,6},{2,0},{4,2},{6,4},{8,14},{10,8},{12,10},{14,12},{16,22},{18,... | collective-permute-start | bytes 2359304 | tf_op jit(solution)/shard_map/panel_ring/ppermute | solution.py:29
  30.0 17.8 %collective-permute-start.9 = (bf16[96,4096]{1,0:T(8,128)(2,1)S(1)}, bf16[96,4096]{1,0:T(8,128)(2,1)S(1)}, u32[]{:S(2)}, u32[]{:S(2)}) collective-permute-start(bf16[96,4096]{1,0:T(8,128)(2,1)S(1)} %pad_maximum_fusion.1.refs_0_), channel_id=1, source_target_pairs={{0,2},{2,4},{4,6},{6,0},{8,10},{10,12},{12,14},{14,8},{16,18},{18,... | collective-permute-start | bytes 2359304 | tf_op jit(solution)/shard_map/panel_ring/ppermute | solution.py:29
  30.0 17.8 %collective-permute-start.12 = (bf16[384,1024]{1,0:T(8,128)(2,1)S(1)}, bf16[384,1024]{1,0:T(8,128)(2,1)S(1)}, u32[]{:S(2)}, u32[]{:S(2)}) collective-permute-start(bf16[384,1024]{1,0:T(8,128)(2,1)S(1)} %constant_dynamic-update-slice_fusion), channel_id=1, source_target_pairs={{0,1},{1,64},{64,65},{65,0},{2,3},{3,66},{66,67},{67,2},{4,5},{5,6... | collective-permute-start | bytes 2359304 | tf_op jit(solution)/shard_map/columns_near/ppermute | solution.py:18
  40.3 12.2 %collective-permute-start.17 = (bf16[192,1024]{1,0:T(8,128)(2,1)S(1)}, bf16[192,1024]{1,0:T(8,128)(2,1)S(1)}, u32[]{:S(2)}, u32[]{:S(2)}) collective-permute-start(bf16[192,1024]{1,0:T(8,128)(2,1)S(1)} %slice.41), channel_id=1, source_target_pairs={{0,65},{1,0},{64,1},{65,64},{2,67},{3,2},{66,3},{67,66},{4,69},{5,... | collective-permute-start | bytes 1179656 | tf_op jit(solution)/shard_map/columns_far/ppermute | solution.py:18
  48.0 13.7 %collective-permute-start.15 = (bf16[384,1024]{1,0:T(8,128)(2,1)S(1)}, bf16[384,1024]{1,0:T(8,128)(2,1)S(1)}, u32[]{:S(2)}, u32[]{:S(2)}) collective-permute-start(bf16[384,1024]{1,0:T(8,128)(2,1)S(1)} %get-tuple-element.66.refs_0_), channel_id=1, source_target_pairs={{0,24},{2,26},{4,28},{6,30},{8,0},{10,2},{12,4},{14,6},{16,8},{18,... | collective-permute-start | bytes 2359304 | tf_op jit(solution)/shard_map/near0/ppermute | solution.py:29
  49.8 12.3 %collective-permute-start.14 = (bf16[384,1024]{1,0:T(8,128)(2,1)S(1)}, bf16[384,1024]{1,0:T(8,128)(2,1)S(1)}, u32[]{:S(2)}, u32[]{:S(2)}) collective-permute-start(bf16[384,1024]{1,0:T(8,128)(2,1)S(1)} %get-tuple-element.66.refs_0_), channel_id=1, source_target_pairs={{0,8},{2,10},{4,12},{6,14},{8,16},{10,18},{12,20},{14,22},{16,24},... | collective-permute-start | bytes 2359304 | tf_op jit(solution)/shard_map/near0/ppermute | solution.py:29
  49.8 32.7 %collective-permute-start.21 = (bf16[384,1536]{1,0:T(8,128)(2,1)S(1)}, bf16[384,1536]{1,0:T(8,128)(2,1)S(1)}, u32[]{:S(2)}, u32[]{:S(2)}) collective-permute-start(bf16[384,1536]{1,0:T(8,128)(2,1)S(1)} %get-tuple-element.71.refs_0_), channel_id=1, source_target_pairs={{0,24},{2,26},{4,28},{6,30},{8,0},{10,2},{12,4},{14,6},{16,8},{18,... | collective-permute-start | bytes 3538952 | tf_op jit(solution)/shard_map/near1/ppermute | solution.py:29
  52.5 30.0 %collective-permute-start.20 = (bf16[384,1536]{1,0:T(8,128)(2,1)S(1)}, bf16[384,1536]{1,0:T(8,128)(2,1)S(1)}, u32[]{:S(2)}, u32[]{:S(2)}) collective-permute-start(bf16[384,1536]{1,0:T(8,128)(2,1)S(1)} %get-tuple-element.71.refs_0_), channel_id=1, source_target_pairs={{0,8},{2,10},{4,12},{6,14},{8,16},{10,18},{12,20},{14,22},{16,24},... | collective-permute-start | bytes 3538952 | tf_op jit(solution)/shard_map/near1/ppermute | solution.py:29
  62.2 14.1 %collective-permute-start.19 = (bf16[192,1024]{1,0:T(8,128)(2,1)S(1)}, bf16[192,1024]{1,0:T(8,128)(2,1)S(1)}, u32[]{:S(2)}, u32[]{:S(2)}) collective-permute-start(bf16[192,1024]{1,0:T(8,128)(2,1)S(1)} %slice.33), channel_id=1, source_target_pairs={{0,24},{2,26},{4,28},{6,30},{8,0},{10,2},{12,4},{14,6},{16,8},{18,... | collective-permute-start | bytes 1179656 | tf_op jit(solution)/shard_map/far0/ppermute | solution.py:29
  65.0 14.0 %collective-permute-start.18 = (bf16[192,1024]{1,0:T(8,128)(2,1)S(1)}, bf16[192,1024]{1,0:T(8,128)(2,1)S(1)}, u32[]{:S(2)}, u32[]{:S(2)}) collective-permute-start(bf16[192,1024]{1,0:T(8,128)(2,1)S(1)} %slice.32), channel_id=1, source_target_pairs={{0,8},{2,10},{4,12},{6,14},{8,16},{10,18},{12,20},{14,22},{16,24},... | collective-permute-start | bytes 1179656 | tf_op jit(solution)/shard_map/far0/ppermute | solution.py:29
  88.2 21.6 %collective-permute-start.26 = (bf16[384,1024]{1,0:T(8,128)(2,1)S(1)}, bf16[384,1024]{1,0:T(8,128)(2,1)S(1)}, u32[]{:S(2)}, u32[]{:S(2)}) collective-permute-start(bf16[384,1024]{1,0:T(8,128)(2,1)S(1)} %get-tuple-element.78.refs_0_), channel_id=1, source_target_pairs={{0,24},{2,26},{4,28},{6,30},{8,0},{10,2},{12,4},{14,6},{16,8},{18,... | collective-permute-start | bytes 2359304 | tf_op jit(solution)/shard_map/near2/ppermute | solution.py:29
  89.9 19.8 %collective-permute-start.25 = (bf16[384,1024]{1,0:T(8,128)(2,1)S(1)}, bf16[384,1024]{1,0:T(8,128)(2,1)S(1)}, u32[]{:S(2)}, u32[]{:S(2)}) collective-permute-start(bf16[384,1024]{1,0:T(8,128)(2,1)S(1)} %get-tuple-element.78.refs_0_), channel_id=1, source_target_pairs={{0,8},{2,10},{4,12},{6,14},{8,16},{10,18},{12,20},{14,22},{16,24},... | collective-permute-start | bytes 2359304 | tf_op jit(solution)/shard_map/near2/ppermute | solution.py:29
  92.2 28.5 %collective-permute-start.31 = (bf16[1024,512]{1,0:T(8,128)(2,1)S(1)}, bf16[1024,512]{1,0:T(8,128)(2,1)S(1)}, u32[]{:S(2)}, u32[]{:S(2)}) collective-permute-start(bf16[1024,512]{1,0:T(8,128)(2,1)S(1)} %get-tuple-element.99), channel_id=1, source_target_pairs={{1,32},{32,1},{3,34},{34,3},{5,36},{36,5},{7,38},{38,7},{9,40},{40... | collective-permute-start | bytes 3145736 | tf_op jit(solution)/shard_map/swap0/ppermute | solution.py:223
  94.2 11.5 %collective-permute-start.24 = (bf16[192,1536]{1,0:T(8,128)(2,1)S(1)}, bf16[192,1536]{1,0:T(8,128)(2,1)S(1)}, u32[]{:S(2)}, u32[]{:S(2)}) collective-permute-start(bf16[192,1536]{1,0:T(8,128)(2,1)S(1)} %slice.35), channel_id=1, source_target_pairs={{0,24},{2,26},{4,28},{6,30},{8,0},{10,2},{12,4},{14,6},{16,8},{18,... | collective-permute-start | bytes 1769480 | tf_op jit(solution)/shard_map/far1/ppermute | solution.py:29
  96.4 11.9 %collective-permute-start.23 = (bf16[192,1536]{1,0:T(8,128)(2,1)S(1)}, bf16[192,1536]{1,0:T(8,128)(2,1)S(1)}, u32[]{:S(2)}, u32[]{:S(2)}) collective-permute-start(bf16[192,1536]{1,0:T(8,128)(2,1)S(1)} %slice.34), channel_id=1, source_target_pairs={{0,8},{2,10},{4,12},{6,14},{8,16},{10,18},{12,20},{14,22},{16,24},... | collective-permute-start | bytes 1769480 | tf_op jit(solution)/shard_map/far1/ppermute | solution.py:29
  109.9 9.6 %collective-permute-start.28 = (bf16[192,1024]{1,0:T(8,128)(2,1)S(1)}, bf16[192,1024]{1,0:T(8,128)(2,1)S(1)}, u32[]{:S(2)}, u32[]{:S(2)}) collective-permute-start(bf16[192,1024]{1,0:T(8,128)(2,1)S(1)} %slice.37), channel_id=1, source_target_pairs={{0,24},{2,26},{4,28},{6,30},{8,0},{10,2},{12,4},{14,6},{16,8},{18,... | collective-permute-start | bytes 1179656 | tf_op jit(solution)/shard_map/far2/ppermute | solution.py:29
  111.4 9.3 %collective-permute-start.27 = (bf16[192,1024]{1,0:T(8,128)(2,1)S(1)}, bf16[192,1024]{1,0:T(8,128)(2,1)S(1)}, u32[]{:S(2)}, u32[]{:S(2)}) collective-permute-start(bf16[192,1024]{1,0:T(8,128)(2,1)S(1)} %slice.36), channel_id=1, source_target_pairs={{0,8},{2,10},{4,12},{6,14},{8,16},{10,18},{12,20},{14,22},{16,24},... | collective-permute-start | bytes 1179656 | tf_op jit(solution)/shard_map/far2/ppermute | solution.py:29
  122.2 9.2 %collective-permute-start.34 = (bf16[192,512]{1,0:T(8,128)(2,1)S(1)}, bf16[192,512]{1,0:T(8,128)(2,1)S(1)}, u32[]{:S(2)}, u32[]{:S(2)}) collective-permute-start(bf16[192,512]{1,0:T(8,128)(2,1)S(1)} %slice.39), channel_id=1, source_target_pairs={{0,24},{2,26},{4,28},{6,30},{8,0},{10,2},{12,4},{14,6},{16,8},{18,... | collective-permute-start | bytes 589832 | tf_op jit(solution)/shard_map/far3/ppermute | solution.py:29
  125.8 21.7 %collective-permute-start.36 = (bf16[1536,512]{1,0:T(8,128)(2,1)S(1)}, bf16[1536,512]{1,0:T(8,128)(2,1)S(1)}, u32[]{:S(2)}, u32[]{:S(2)}) collective-permute-start(bf16[1536,512]{1,0:T(8,128)(2,1)S(1)} %get-tuple-element.97), channel_id=1, source_target_pairs={{1,32},{32,1},{3,34},{34,3},{5,36},{36,5},{7,38},{38,7},{9,40},{40... | collective-permute-start | bytes 4718600 | tf_op jit(solution)/shard_map/swap1/ppermute | solution.py:223
  148.7 16.4 %collective-permute-start.39 = (bf16[1024,512]{1,0:T(8,128)(2,1)}, bf16[1024,512]{1,0:T(8,128)(2,1)}, u32[]{:S(2)}, u32[]{:S(2)}) collective-permute-start(bf16[1024,512]{1,0:T(8,128)(2,1)} %get-tuple-element.95), channel_id=1, source_target_pairs={{1,32},{32,1},{3,34},{34,3},{5,36},{36,5},{7,38},{38,7},{9,40},{40... | collective-permute-start | bytes 3145736 | tf_op jit(solution)/shard_map/swap2/ppermute | solution.py:223
  152.0 18.7 %collective-permute-start.38 = (bf16[512,512]{1,0:T(8,128)(2,1)}, bf16[512,512]{1,0:T(8,128)(2,1)}, u32[]{:S(2)}, u32[]{:S(2)}) collective-permute-start(bf16[512,512]{1,0:T(8,128)(2,1)} %get-tuple-element.93), channel_id=1, source_target_pairs={{1,32},{32,1},{3,34},{34,3},{5,36},{36,5},{7,38},{38,7},{9,40},{40... | collective-permute-start | bytes 1572872 | tf_op jit(solution)/shard_map/swap3/ppermute | solution.py:223
  (24 other events, 128.3 us)

commit v3 on v2

--- a/solution.py
+++ b/solution.py
@@ -206,16 +206,16 @@
         with jax.named_scope(f"product{n}"):
             mine, other = products(near[n] + far[n], columns)
         gate = []
-        if n == 0:
-            gate += near[1][1:]
-        elif n < last:
+        if n < last:
             gate += far[n + 1]
         if 0 < n and n + 1 < last:
             gate += near[n + 2][1:]
         if n > 0:
             gate.append(sent[n - 1])
+        if n > 0:
             gate.append(sums[max(n - 2, 0)][1])
-        other, _ = lax.optimization_barrier((other, gate))
+        if gate:
+            other, _ = lax.optimization_barrier((other, gate))
         with jax.named_scope(f"exchange{n}"):
             mine = mine + core_swap(other).astype(jnp.float32)
             sent.append(mine.astype(jnp.bfloat16))

time: 174 us -> 171 us (0.983)
  waiting for transfers between devices: 75.5 us -> 72.6 us
    ppermute x25, waiting for transfers between devices: 36 us -> 32.9 us  [ring_shift(): return lax.ppermute(value, ('c', 'y', 'x'), table)]
  transfers between devices with their start and end apart: 40 -> 40, of which waited for: 20 -> 21; matrix products, arithmetic and copies ran while one was open for 4% -> 4% of each run, Pallas kernels for 12% -> 12%
where the time goes in v3:
time: 171 us
  waiting for transfers between devices  72.6 us (42%)
  starting transfers between devices  58.9 us (34%)
  Pallas kernels  24 us (14%)
  other arithmetic  7.28 us (4%)
  local copies, waits for them, and re-layouts  7.2 us (4%)
    ppermute x25, waiting for transfers between devices, ring_shift(): return lax.ppermute(value, ('c', 'y', 'x'), table)  32.9 us
    ppermute x25, starting transfers between devices, ring_shift(): return lax.ppermute(value, ('c', 'y', 'x'), table)  30.4 us
    ppermute x7, waiting for transfers between devices, z_shift(): lax.ppermute(value, ('zh', 'zl'), [(z, (z + step) % 4) for z in range(4)])  20.4 us
    ppermute x4, waiting for transfers between devices, on_device(): sums.append((mine, lax.ppermute(sent[n], ('c', 'zl'), [(1, 2), (2, 1)])))  16.5 us
    pallas_call x7, Pallas kernels, in_vmem(): pl.pallas_call(kernel, out_shape=outs, in_specs=[pl.BlockSpec(memory_spac...  15.5 us
    ppermute x7, starting transfers between devices, z_shift(): lax.ppermute(value, ('zh', 'zl'), [(z, (z + step) % 4) for z in range(4)])  12.4 us
    ppermute x4, starting transfers between devices, on_device(): sums.append((mine, lax.ppermute(sent[n], ('c', 'zl'), [(1, 2), (2, 1)])))  9.59 us
    pallas_call x4, Pallas kernels, write_out(): pl.pallas_call(kernel, out_shape=shape_of(total, cols, jnp.float32), in_s...  8.51 us
  transfers between devices with their start and end apart: 40, of which 21 were waited for; matrix products, arithmetic and copies ran while one was open for 4% of the time, Pallas kernels for 12%

profile of v3, /device:TPU:1, one launch (start us, length us, event | category | flops | bytes accessed | tf_op | source)
XLA Modules:
  0.0 170.5 jit_solution(13958535872035783827)
XLA Ops:
  3.1 2.2 %collective-permute-start.3 = (bf16[24,4096]{1,0:T(8,128)(2,1)S(1)}, bf16[24,4096]{1,0:T(8,128)(2,1)S(1)}, u32[]{:S(2)}, u32[]{:S(2)}) collective-permute-start(bf16[24,4096]{1,0:T(8,128)(2,1)S(1)} %get-tuple-element.54), channel_id=1, source_target_pairs={{0,2},{2,4},{4,6},{6,0},{8,10},{10,12},{12,14},{14,8},{16,18},{18,... | collective-permute-start | bytes 589832 | tf_op jit(solution)/shard_map/columns_first/ppermute | solution.py:29
  17.1 3.1 %collective-permute-start.8 = (bf16[96,1024]{1,0:T(8,128)(2,1)S(1)}, bf16[96,1024]{1,0:T(8,128)(2,1)S(1)}, u32[]{:S(2)}, u32[]{:S(2)}) collective-permute-start(bf16[96,1024]{1,0:T(8,128)(2,1)S(1)} %get-tuple-element.60), channel_id=1, source_target_pairs={{0,16},{2,18},{4,20},{6,22},{8,24},{10,26},{12,28},{14,30},{16,0},... | collective-permute-start | bytes 589832 | tf_op jit(solution)/shard_map/columns_second/ppermute | solution.py:29
  23.2 3.5 %collective-permute-start.13 = (bf16[384,1024]{1,0:T(8,128)(2,1)S(1)}, bf16[384,1024]{1,0:T(8,128)(2,1)S(1)}, u32[]{:S(2)}, u32[]{:S(2)}) collective-permute-start(bf16[384,1024]{1,0:T(8,128)(2,1)S(1)} %constant_dynamic-update-slice_fusion), channel_id=1, source_target_pairs={{0,65},{1,0},{64,1},{65,64},{2,67},{3,2},{66,3},{67,66},{4,69},{5,... | collective-permute-start | bytes 2359304 | tf_op jit(solution)/shard_map/columns_near/ppermute | solution.py:18
  30.0 10.3 %collective-permute-done.13 = bf16[384,1024]{1,0:T(8,128)(2,1)S(1)} collective-permute-done((bf16[384,1024]{1,0:T(8,128)(2,1)S(1)}, bf16[384,1024]{1,0:T(8,128)(2,1)S(1)}, u32[]{:S(2)}, u32[]{:S(2)}) %collective-permute-start.13) | collective-permute-done | bytes 786464 | tf_op jit(solution)/shard_map/columns_near/ppermute | solution.py:18
  40.3 3.5 %collective-permute-start.17 = (bf16[192,1024]{1,0:T(8,128)(2,1)S(1)}, bf16[192,1024]{1,0:T(8,128)(2,1)S(1)}, u32[]{:S(2)}, u32[]{:S(2)}) collective-permute-start(bf16[192,1024]{1,0:T(8,128)(2,1)S(1)} %slice.41), channel_id=1, source_target_pairs={{0,65},{1,0},{64,1},{65,64},{2,67},{3,2},{66,3},{67,66},{4,69},{5,... | collective-permute-start | bytes 1179656 | tf_op jit(solution)/shard_map/columns_far/ppermute | solution.py:18
  43.8 3.3 %collective-permute-done.10.refs_2_ = bf16[96,4096]{1,0:T(8,128)(2,1)S(1)} collective-permute-done((bf16[96,4096]{1,0:T(8,128)(2,1)S(1)}, bf16[96,4096]{1,0:T(8,128)(2,1)S(1)}, u32[]{:S(2)}, u32[]{:S(2)}) %collective-permute-start.10) | collective-permute-done | bytes 786464 | tf_op jit(solution)/shard_map/panel_ring/ppermute | solution.py:29
  49.8 2.7 %collective-permute-start.21 = (bf16[384,1536]{1,0:T(8,128)(2,1)S(1)}, bf16[384,1536]{1,0:T(8,128)(2,1)S(1)}, u32[]{:S(2)}, u32[]{:S(2)}) collective-permute-start(bf16[384,1536]{1,0:T(8,128)(2,1)S(1)} %get-tuple-element.71.refs_0_), channel_id=1, source_target_pairs={{0,24},{2,26},{4,28},{6,30},{8,0},{10,2},{12,4},{14,6},{16,8},{18,... | collective-permute-start | bytes 3538952 | tf_op jit(solution)/shard_map/near1/ppermute | solution.py:29
  52.6 9.1 %collective-permute-done.16 = bf16[192,1024]{1,0:T(8,128)(2,1)S(1)} collective-permute-done((bf16[192,1024]{1,0:T(8,128)(2,1)S(1)}, bf16[192,1024]{1,0:T(8,128)(2,1)S(1)}, u32[]{:S(2)}, u32[]{:S(2)}) %collective-permute-start.16) | collective-permute-done | bytes 393248 | tf_op jit(solution)/shard_map/columns_far/ppermute | solution.py:18
  62.2 2.8 %collective-permute-start.19 = (bf16[192,1024]{1,0:T(8,128)(2,1)S(1)}, bf16[192,1024]{1,0:T(8,128)(2,1)S(1)}, u32[]{:S(2)}, u32[]{:S(2)}) collective-permute-start(bf16[192,1024]{1,0:T(8,128)(2,1)S(1)} %slice.33), channel_id=1, source_target_pairs={{0,24},{2,26},{4,28},{6,30},{8,0},{10,2},{12,4},{14,6},{16,8},{18,... | collective-permute-start | bytes 1179656 | tf_op jit(solution)/shard_map/far0/ppermute | solution.py:29
  65.0 11.3 %collective-permute-done.19.refs_4_ = bf16[192,1024]{1,0:T(8,128)(2,1)S(1)} collective-permute-done((bf16[192,1024]{1,0:T(8,128)(2,1)S(1)}, bf16[192,1024]{1,0:T(8,128)(2,1)S(1)}, u32[]{:S(2)}, u32[]{:S(2)}) %collective-permute-start.19) | collective-permute-done | bytes 393248 | tf_op jit(solution)/shard_map/far0/ppermute | solution.py:29
  76.3 2.7 %collective-permute-done.18.refs_3_ = bf16[192,1024]{1,0:T(8,128)(2,1)S(1)} collective-permute-done((bf16[192,1024]{1,0:T(8,128)(2,1)S(1)}, bf16[192,1024]{1,0:T(8,128)(2,1)S(1)}, u32[]{:S(2)}, u32[]{:S(2)}) %collective-permute-start.18) | collective-permute-done | bytes 393248 | tf_op jit(solution)/shard_map/far0/ppermute | solution.py:29
  81.2 3.5 %product0.1 = (f32[1024,512]{1,0:T(8,128)S(1)}, bf16[1024,512]{1,0:T(8,128)(2,1)S(1)}) custom-call(bf16[384,1024]{1,0:T(8,128)(2,1)S(1)} %get-tuple-element.66.refs_0_, bf16[384,1024]{1,0:T(8,128)(2,1)S(1)} %collective-permute-done.14.refs_1_, bf16[384,1024]{1,0:T(8,128)(2,1)S(1)} %collective-permute-done.15.refs_2_, ...), custom_call_target="tpu_custom_call" | custom-call | tf_op jit(solution)/shard_map/product0/pallas_call | solution.py:33
  84.6 3.6 %collective-permute-done.23.refs_4_ = bf16[192,1536]{1,0:T(8,128)(2,1)S(1)} collective-permute-done((bf16[192,1536]{1,0:T(8,128)(2,1)S(1)}, bf16[192,1536]{1,0:T(8,128)(2,1)S(1)}, u32[]{:S(2)}, u32[]{:S(2)}) %collective-permute-start.23) | collective-permute-done | bytes 589856 | tf_op jit(solution)/shard_map/far1/ppermute | solution.py:29
  89.7 6.3 %collective-permute-start.24 = (bf16[1024,512]{1,0:T(8,128)(2,1)S(1)}, bf16[1024,512]{1,0:T(8,128)(2,1)S(1)}, u32[]{:S(2)}, u32[]{:S(2)}) collective-permute-start(bf16[1024,512]{1,0:T(8,128)(2,1)S(1)} %get-tuple-element.74), channel_id=1, source_target_pairs={{0,32},{32,0},{1,33},{33,1},{2,34},{34,2},{3,35},{35,3},{4,36},{36... | collective-permute-start | bytes 3145736 | tf_op jit(solution)/shard_map/exchange0/ppermute | solution.py:125
  101.9 2.2 %collective-permute-start.30 = (bf16[384,512]{1,0:T(8,128)(2,1)S(1)}, bf16[384,512]{1,0:T(8,128)(2,1)S(1)}, u32[]{:S(2)}, u32[]{:S(2)}) collective-permute-start(bf16[384,512]{1,0:T(8,128)(2,1)S(1)} %get-tuple-element.82.refs_0_), channel_id=1, source_target_pairs={{0,24},{2,26},{4,28},{6,30},{8,0},{10,2},{12,4},{14,6},{16,8},{18,... | collective-permute-start | bytes 1179656 | tf_op jit(solution)/shard_map/near3/ppermute | solution.py:29
  104.1 3.0 %collective-permute-done.26.refs_2_ = bf16[384,1024]{1,0:T(8,128)(2,1)S(1)} collective-permute-done((bf16[384,1024]{1,0:T(8,128)(2,1)S(1)}, bf16[384,1024]{1,0:T(8,128)(2,1)S(1)}, u32[]{:S(2)}, u32[]{:S(2)}) %collective-permute-start.26) | collective-permute-done | bytes 786464 | tf_op jit(solution)/shard_map/near2/ppermute | solution.py:29
  107.1 2.9 %collective-permute-done.25.refs_1_ = bf16[384,1024]{1,0:T(8,128)(2,1)S(1)} collective-permute-done((bf16[384,1024]{1,0:T(8,128)(2,1)S(1)}, bf16[384,1024]{1,0:T(8,128)(2,1)S(1)}, u32[]{:S(2)}, u32[]{:S(2)}) %collective-permute-start.25) | collective-permute-done | bytes 786464 | tf_op jit(solution)/shard_map/near2/ppermute | solution.py:29
  111.7 5.1 %product1.1 = (f32[1536,512]{1,0:T(8,128)S(1)}, bf16[1536,512]{1,0:T(8,128)(2,1)S(1)}) custom-call(bf16[384,1536]{1,0:T(8,128)(2,1)S(1)} %get-tuple-element.71.refs_0_, bf16[384,1536]{1,0:T(8,128)(2,1)S(1)} %collective-permute-done.20.refs_1_, bf16[384,1536]{1,0:T(8,128)(2,1)S(1)} %collective-permute-done.21.refs_2_, ...), custom_call_target="tpu_custom_call" | custom-call | tf_op jit(solution)/shard_map/product1/pallas_call | solution.py:33
  125.4 3.5 %product2.1 = (f32[1024,512]{1,0:T(8,128)S(1)}, bf16[1024,512]{1,0:T(8,128)(2,1)S(1)}) custom-call(bf16[384,1024]{1,0:T(8,128)(2,1)S(1)} %get-tuple-element.78.refs_0_, bf16[384,1024]{1,0:T(8,128)(2,1)S(1)} %collective-permute-done.25.refs_1_, bf16[384,1024]{1,0:T(8,128)(2,1)S(1)} %collective-permute-done.26.refs_2_, ...), custom_call_target="tpu_custom_call" | custom-call | tf_op jit(solution)/shard_map/product2/pallas_call | solution.py:33
  133.7 11.3 %collective-permute-done.36.moved_ref = bf16[1536,512]{1,0:T(8,128)(2,1)S(1)} collective-permute-done((bf16[1536,512]{1,0:T(8,128)(2,1)S(1)}, bf16[1536,512]{1,0:T(8,128)(2,1)S(1)}, u32[]{:S(2)}, u32[]{:S(2)}) %collective-permute-start.36) | collective-permute-done | bytes 1572896 | tf_op jit(solution)/shard_map/swap1/ppermute | solution.py:223
  149.5 3.6 %collective-permute-start.38 = (bf16[512,512]{1,0:T(8,128)(2,1)}, bf16[512,512]{1,0:T(8,128)(2,1)}, u32[]{:S(2)}, u32[]{:S(2)}) collective-permute-start(bf16[512,512]{1,0:T(8,128)(2,1)} %get-tuple-element.93), channel_id=1, source_target_pairs={{1,32},{32,1},{3,34},{34,3},{5,36},{36,5},{7,38},{38,7},{9,40},{40... | collective-permute-start | bytes 1572872 | tf_op jit(solution)/shard_map/swap3/ppermute | solution.py:223
  160.1 2.5 %collective-permute-done.39.moved_ref = bf16[1024,512]{1,0:T(8,128)(2,1)} collective-permute-done((bf16[1024,512]{1,0:T(8,128)(2,1)}, bf16[1024,512]{1,0:T(8,128)(2,1)}, u32[]{:S(2)}, u32[]{:S(2)}) %collective-permute-start.39) | collective-permute-done | bytes 1048608 | tf_op jit(solution)/shard_map/swap2/ppermute | solution.py:223
  162.6 2.9 %shard_map.41.refs_0_ = f32[4096,512]{1,0:T(8,128)} custom-call(s32[1]{0:T(128)} %bitcast.stays_ref, f32[1024,512]{1,0:T(8,128)S(1)} %copy-done.1, bf16[1024,512]{1,0:T(8,128)(2,1)} %collective-permute-done.39.moved_ref, f32[4096,512]{1,0:T(8,128)} %shard_map.40.refs_0_), custom_call_target="tpu_custom_call", output_to_operand_aliasing={{}: (3, {})} | custom-call | tf_op jit(solution)/shard_map/pallas_call | solution.py:139
  165.5 2.7 %collective-permute-done.38.moved_ref = bf16[512,512]{1,0:T(8,128)(2,1)} collective-permute-done((bf16[512,512]{1,0:T(8,128)(2,1)}, bf16[512,512]{1,0:T(8,128)(2,1)}, u32[]{:S(2)}, u32[]{:S(2)}) %collective-permute-start.38) | collective-permute-done | bytes 524320 | tf_op jit(solution)/shard_map/swap3/ppermute | solution.py:223
  (108 shorter events, 62.6 us)
Async XLA Ops:
  10.1 10.1 %collective-permute-start.1 = (bf16[24,4096]{1,0:T(8,128)(2,1)S(1)}, bf16[24,4096]{1,0:T(8,128)(2,1)S(1)}, u32[]{:S(2)}, u32[]{:S(2)}) collective-permute-start(bf16[24,4096]{1,0:T(8,128)(2,1)S(1)} %get-tuple-element.51), channel_id=1, source_target_pairs={{0,65},{1,0},{64,1},{65,64},{2,67},{3,2},{66,3},{67,66},{4,69},{5,... | collective-permute-start | bytes 589832 | tf_op jit(solution)/shard_map/panel_z/ppermute | solution.py:18
  23.2 17.0 %collective-permute-start.13 = (bf16[384,1024]{1,0:T(8,128)(2,1)S(1)}, bf16[384,1024]{1,0:T(8,128)(2,1)S(1)}, u32[]{:S(2)}, u32[]{:S(2)}) collective-permute-start(bf16[384,1024]{1,0:T(8,128)(2,1)S(1)} %constant_dynamic-update-slice_fusion), channel_id=1, source_target_pairs={{0,65},{1,0},{64,1},{65,64},{2,67},{3,2},{66,3},{67,66},{4,69},{5,... | collective-permute-start | bytes 2359304 | tf_op jit(solution)/shard_map/columns_near/ppermute | solution.py:18
  26.8 17.0 %collective-permute-start.11 = (bf16[96,4096]{1,0:T(8,128)(2,1)S(1)}, bf16[96,4096]{1,0:T(8,128)(2,1)S(1)}, u32[]{:S(2)}, u32[]{:S(2)}) collective-permute-start(bf16[96,4096]{1,0:T(8,128)(2,1)S(1)} %pad_maximum_fusion.1.refs_0_), channel_id=1, source_target_pairs={{0,4},{2,6},{4,0},{6,2},{8,12},{10,14},{12,8},{14,10},{16,20},{18,... | collective-permute-start | bytes 2359304 | tf_op jit(solution)/shard_map/panel_ring/ppermute | solution.py:29
  28.1 19.0 %collective-permute-start.10 = (bf16[96,4096]{1,0:T(8,128)(2,1)S(1)}, bf16[96,4096]{1,0:T(8,128)(2,1)S(1)}, u32[]{:S(2)}, u32[]{:S(2)}) collective-permute-start(bf16[96,4096]{1,0:T(8,128)(2,1)S(1)} %pad_maximum_fusion.1.refs_0_), channel_id=1, source_target_pairs={{0,6},{2,0},{4,2},{6,4},{8,14},{10,8},{12,10},{14,12},{16,22},{18,... | collective-permute-start | bytes 2359304 | tf_op jit(solution)/shard_map/panel_ring/ppermute | solution.py:29
  30.0 17.8 %collective-permute-start.9 = (bf16[96,4096]{1,0:T(8,128)(2,1)S(1)}, bf16[96,4096]{1,0:T(8,128)(2,1)S(1)}, u32[]{:S(2)}, u32[]{:S(2)}) collective-permute-start(bf16[96,4096]{1,0:T(8,128)(2,1)S(1)} %pad_maximum_fusion.1.refs_0_), channel_id=1, source_target_pairs={{0,2},{2,4},{4,6},{6,0},{8,10},{10,12},{12,14},{14,8},{16,18},{18,... | collective-permute-start | bytes 2359304 | tf_op jit(solution)/shard_map/panel_ring/ppermute | solution.py:29
  30.0 17.8 %collective-permute-start.12 = (bf16[384,1024]{1,0:T(8,128)(2,1)S(1)}, bf16[384,1024]{1,0:T(8,128)(2,1)S(1)}, u32[]{:S(2)}, u32[]{:S(2)}) collective-permute-start(bf16[384,1024]{1,0:T(8,128)(2,1)S(1)} %constant_dynamic-update-slice_fusion), channel_id=1, source_target_pairs={{0,1},{1,64},{64,65},{65,0},{2,3},{3,66},{66,67},{67,2},{4,5},{5,6... | collective-permute-start | bytes 2359304 | tf_op jit(solution)/shard_map/columns_near/ppermute | solution.py:18
  40.3 12.2 %collective-permute-start.17 = (bf16[192,1024]{1,0:T(8,128)(2,1)S(1)}, bf16[192,1024]{1,0:T(8,128)(2,1)S(1)}, u32[]{:S(2)}, u32[]{:S(2)}) collective-permute-start(bf16[192,1024]{1,0:T(8,128)(2,1)S(1)} %slice.41), channel_id=1, source_target_pairs={{0,65},{1,0},{64,1},{65,64},{2,67},{3,2},{66,3},{67,66},{4,69},{5,... | collective-permute-start | bytes 1179656 | tf_op jit(solution)/shard_map/columns_far/ppermute | solution.py:18
  48.0 13.7 %collective-permute-start.15 = (bf16[384,1024]{1,0:T(8,128)(2,1)S(1)}, bf16[384,1024]{1,0:T(8,128)(2,1)S(1)}, u32[]{:S(2)}, u32[]{:S(2)}) collective-permute-start(bf16[384,1024]{1,0:T(8,128)(2,1)S(1)} %get-tuple-element.66.refs_0_), channel_id=1, source_target_pairs={{0,24},{2,26},{4,28},{6,30},{8,0},{10,2},{12,4},{14,6},{16,8},{18,... | collective-permute-start | bytes 2359304 | tf_op jit(solution)/shard_map/near0/ppermute | solution.py:29
  49.8 12.3 %collective-permute-start.14 = (bf16[384,1024]{1,0:T(8,128)(2,1)S(1)}, bf16[384,1024]{1,0:T(8,128)(2,1)S(1)}, u32[]{:S(2)}, u32[]{:S(2)}) collective-permute-start(bf16[384,1024]{1,0:T(8,128)(2,1)S(1)} %get-tuple-element.66.refs_0_), channel_id=1, source_target_pairs={{0,8},{2,10},{4,12},{6,14},{8,16},{10,18},{12,20},{14,22},{16,24},... | collective-permute-start | bytes 2359304 | tf_op jit(solution)/shard_map/near0/ppermute | solution.py:29
  49.8 29.2 %collective-permute-start.21 = (bf16[384,1536]{1,0:T(8,128)(2,1)S(1)}, bf16[384,1536]{1,0:T(8,128)(2,1)S(1)}, u32[]{:S(2)}, u32[]{:S(2)}) collective-permute-start(bf16[384,1536]{1,0:T(8,128)(2,1)S(1)} %get-tuple-element.71.refs_0_), channel_id=1, source_target_pairs={{0,24},{2,26},{4,28},{6,30},{8,0},{10,2},{12,4},{14,6},{16,8},{18,... | collective-permute-start | bytes 3538952 | tf_op jit(solution)/shard_map/near1/ppermute | solution.py:29
  52.5 26.5 %collective-permute-start.20 = (bf16[384,1536]{1,0:T(8,128)(2,1)S(1)}, bf16[384,1536]{1,0:T(8,128)(2,1)S(1)}, u32[]{:S(2)}, u32[]{:S(2)}) collective-permute-start(bf16[384,1536]{1,0:T(8,128)(2,1)S(1)} %get-tuple-element.71.refs_0_), channel_id=1, source_target_pairs={{0,8},{2,10},{4,12},{6,14},{8,16},{10,18},{12,20},{14,22},{16,24},... | collective-permute-start | bytes 3538952 | tf_op jit(solution)/shard_map/near1/ppermute | solution.py:29
  52.6 9.2 %collective-permute-start.16 = (bf16[192,1024]{1,0:T(8,128)(2,1)S(1)}, bf16[192,1024]{1,0:T(8,128)(2,1)S(1)}, u32[]{:S(2)}, u32[]{:S(2)}) collective-permute-start(bf16[192,1024]{1,0:T(8,128)(2,1)S(1)} %slice.40), channel_id=1, source_target_pairs={{0,1},{1,64},{64,65},{65,0},{2,3},{3,66},{66,67},{67,2},{4,5},{5,6... | collective-permute-start | bytes 1179656 | tf_op jit(solution)/shard_map/columns_far/ppermute | solution.py:18
  62.2 14.1 %collective-permute-start.19 = (bf16[192,1024]{1,0:T(8,128)(2,1)S(1)}, bf16[192,1024]{1,0:T(8,128)(2,1)S(1)}, u32[]{:S(2)}, u32[]{:S(2)}) collective-permute-start(bf16[192,1024]{1,0:T(8,128)(2,1)S(1)} %slice.33), channel_id=1, source_target_pairs={{0,24},{2,26},{4,28},{6,30},{8,0},{10,2},{12,4},{14,6},{16,8},{18,... | collective-permute-start | bytes 1179656 | tf_op jit(solution)/shard_map/far0/ppermute | solution.py:29
  65.0 14.0 %collective-permute-start.18 = (bf16[192,1024]{1,0:T(8,128)(2,1)S(1)}, bf16[192,1024]{1,0:T(8,128)(2,1)S(1)}, u32[]{:S(2)}, u32[]{:S(2)}) collective-permute-start(bf16[192,1024]{1,0:T(8,128)(2,1)S(1)} %slice.32), channel_id=1, source_target_pairs={{0,8},{2,10},{4,12},{6,14},{8,16},{10,18},{12,20},{14,22},{16,24},... | collective-permute-start | bytes 1179656 | tf_op jit(solution)/shard_map/far0/ppermute | solution.py:29
  79.2 10.5 %collective-permute-start.22 = (bf16[192,1536]{1,0:T(8,128)(2,1)S(1)}, bf16[192,1536]{1,0:T(8,128)(2,1)S(1)}, u32[]{:S(2)}, u32[]{:S(2)}) collective-permute-start(bf16[192,1536]{1,0:T(8,128)(2,1)S(1)} %slice.34), channel_id=1, source_target_pairs={{0,8},{2,10},{4,12},{6,14},{8,16},{10,18},{12,20},{14,22},{16,24},... | collective-permute-start | bytes 1769480 | tf_op jit(solution)/shard_map/far1/ppermute | solution.py:29
  96.0 11.1 %collective-permute-start.26 = (bf16[384,1024]{1,0:T(8,128)(2,1)S(1)}, bf16[384,1024]{1,0:T(8,128)(2,1)S(1)}, u32[]{:S(2)}, u32[]{:S(2)}) collective-permute-start(bf16[384,1024]{1,0:T(8,128)(2,1)S(1)} %get-tuple-element.78.refs_0_), channel_id=1, source_target_pairs={{0,24},{2,26},{4,28},{6,30},{8,0},{10,2},{12,4},{14,6},{16,8},{18,... | collective-permute-start | bytes 2359304 | tf_op jit(solution)/shard_map/near2/ppermute | solution.py:29
  97.7 12.3 %collective-permute-start.25 = (bf16[384,1024]{1,0:T(8,128)(2,1)S(1)}, bf16[384,1024]{1,0:T(8,128)(2,1)S(1)}, u32[]{:S(2)}, u32[]{:S(2)}) collective-permute-start(bf16[384,1024]{1,0:T(8,128)(2,1)S(1)} %get-tuple-element.78.refs_0_), channel_id=1, source_target_pairs={{0,8},{2,10},{4,12},{6,14},{8,16},{10,18},{12,20},{14,22},{16,24},... | collective-permute-start | bytes 2359304 | tf_op jit(solution)/shard_map/near2/ppermute | solution.py:29
  100.0 18.2 %collective-permute-start.31 = (bf16[1024,512]{1,0:T(8,128)(2,1)S(1)}, bf16[1024,512]{1,0:T(8,128)(2,1)S(1)}, u32[]{:S(2)}, u32[]{:S(2)}) collective-permute-start(bf16[1024,512]{1,0:T(8,128)(2,1)S(1)} %get-tuple-element.99), channel_id=1, source_target_pairs={{1,32},{32,1},{3,34},{34,3},{5,36},{36,5},{7,38},{38,7},{9,40},{40... | collective-permute-start | bytes 3145736 | tf_op jit(solution)/shard_map/swap0/ppermute | solution.py:223
  101.9 14.8 %collective-permute-start.30 = (bf16[384,512]{1,0:T(8,128)(2,1)S(1)}, bf16[384,512]{1,0:T(8,128)(2,1)S(1)}, u32[]{:S(2)}, u32[]{:S(2)}) collective-permute-start(bf16[384,512]{1,0:T(8,128)(2,1)S(1)} %get-tuple-element.82.refs_0_), channel_id=1, source_target_pairs={{0,24},{2,26},{4,28},{6,30},{8,0},{10,2},{12,4},{14,6},{16,8},{18,... | collective-permute-start | bytes 1179656 | tf_op jit(solution)/shard_map/near3/ppermute | solution.py:29
  104.1 12.7 %collective-permute-start.29 = (bf16[384,512]{1,0:T(8,128)(2,1)S(1)}, bf16[384,512]{1,0:T(8,128)(2,1)S(1)}, u32[]{:S(2)}, u32[]{:S(2)}) collective-permute-start(bf16[384,512]{1,0:T(8,128)(2,1)S(1)} %get-tuple-element.82.refs_0_), channel_id=1, source_target_pairs={{0,8},{2,10},{4,12},{6,14},{8,16},{10,18},{12,20},{14,22},{16,24},... | collective-permute-start | bytes 1179656 | tf_op jit(solution)/shard_map/near3/ppermute | solution.py:29
  119.5 9.4 %collective-permute-start.34 = (bf16[192,512]{1,0:T(8,128)(2,1)S(1)}, bf16[192,512]{1,0:T(8,128)(2,1)S(1)}, u32[]{:S(2)}, u32[]{:S(2)}) collective-permute-start(bf16[192,512]{1,0:T(8,128)(2,1)S(1)} %slice.39), channel_id=1, source_target_pairs={{0,24},{2,26},{4,28},{6,30},{8,0},{10,2},{12,4},{14,6},{16,8},{18,... | collective-permute-start | bytes 589832 | tf_op jit(solution)/shard_map/far3/ppermute | solution.py:29
  123.3 21.7 %collective-permute-start.36 = (bf16[1536,512]{1,0:T(8,128)(2,1)S(1)}, bf16[1536,512]{1,0:T(8,128)(2,1)S(1)}, u32[]{:S(2)}, u32[]{:S(2)}) collective-permute-start(bf16[1536,512]{1,0:T(8,128)(2,1)S(1)} %get-tuple-element.97), channel_id=1, source_target_pairs={{1,32},{32,1},{3,34},{34,3},{5,36},{36,5},{7,38},{38,7},{9,40},{40... | collective-permute-start | bytes 4718600 | tf_op jit(solution)/shard_map/swap1/ppermute | solution.py:223
  146.2 16.4 %collective-permute-start.39 = (bf16[1024,512]{1,0:T(8,128)(2,1)}, bf16[1024,512]{1,0:T(8,128)(2,1)}, u32[]{:S(2)}, u32[]{:S(2)}) collective-permute-start(bf16[1024,512]{1,0:T(8,128)(2,1)} %get-tuple-element.95), channel_id=1, source_target_pairs={{1,32},{32,1},{3,34},{34,3},{5,36},{36,5},{7,38},{38,7},{9,40},{40... | collective-permute-start | bytes 3145736 | tf_op jit(solution)/shard_map/swap2/ppermute | solution.py:223
  149.5 18.7 %collective-permute-start.38 = (bf16[512,512]{1,0:T(8,128)(2,1)}, bf16[512,512]{1,0:T(8,128)(2,1)}, u32[]{:S(2)}, u32[]{:S(2)}) collective-permute-start(bf16[512,512]{1,0:T(8,128)(2,1)} %get-tuple-element.93), channel_id=1, source_target_pairs={{1,32},{32,1},{3,34},{34,3},{5,36},{36,5},{7,38},{38,7},{9,40},{40... | collective-permute-start | bytes 1572872 | tf_op jit(solution)/shard_map/swap3/ppermute | solution.py:223
  (24 other events, 127.6 us)

commit v4 on v3

--- a/solution.py
+++ b/solution.py
@@ -212,13 +212,15 @@
             gate += near[n + 2][1:]
         if n > 0:
             gate.append(sent[n - 1])
-        if n > 0:
+        if 0 < n < last:
             gate.append(sums[max(n - 2, 0)][1])
         if gate:
             other, _ = lax.optimization_barrier((other, gate))
         with jax.named_scope(f"exchange{n}"):
             mine = mine + core_swap(other).astype(jnp.float32)
             sent.append(mine.astype(jnp.bfloat16))
+        if n == last:
+            sent[n], _ = lax.optimization_barrier((sent[n], sums[n - 2][1]))
         with jax.named_scope(f"swap{n}"):
             sums.append((mine, lax.ppermute(sent[n], ("c", "zl"), [(1, 2), (2, 1)])))
     stays = (c == zl).astype(jnp.int32).reshape(1)

time: 171 us -> 168 us (0.982)
  waiting for transfers between devices: 72.6 us -> 70.3 us
    ppermute x4, waiting for transfers between devices: 2.74 us -> 0.57 us  [core_swap(): return lax.ppermute(value, 'c', [(0, 1), (1, 0)])]
  transfers between devices with their start and end apart: 40 -> 40, of which waited for: 21 -> 20; matrix products, arithmetic and copies ran while one was open for 4% -> 4% of each run, Pallas kernels for 12% -> 13%
where the time goes in v4:
time: 168 us; the launch traced here: 167 us
  waiting for transfers between devices  70.3 us (42%)
  starting transfers between devices  58.7 us (35%)
  Pallas kernels  24 us (14%)
  other arithmetic  7.34 us (4%)
  local copies, waits for them, and re-layouts  6.15 us (4%)
    ppermute x25, waiting for transfers between devices, ring_shift(): return lax.ppermute(value, ('c', 'y', 'x'), table)  34.5 us
    ppermute x25, starting transfers between devices, ring_shift(): return lax.ppermute(value, ('c', 'y', 'x'), table)  30.4 us
    ppermute x7, waiting for transfers between devices, z_shift(): lax.ppermute(value, ('zh', 'zl'), [(z, (z + step) % 4) for z in range(4)])  20.4 us
    pallas_call x7, Pallas kernels, in_vmem(): pl.pallas_call(kernel, out_shape=outs, in_specs=[pl.BlockSpec(memory_spac...  15.5 us
    ppermute x4, waiting for transfers between devices, on_device(): sums.append((mine, lax.ppermute(sent[n], ('c', 'zl'), [(1, 2), (2, 1)])))  14.8 us
    ppermute x7, starting transfers between devices, z_shift(): lax.ppermute(value, ('zh', 'zl'), [(z, (z + step) % 4) for z in range(4)])  12.4 us
    ppermute x4, starting transfers between devices, on_device(): sums.append((mine, lax.ppermute(sent[n], ('c', 'zl'), [(1, 2), (2, 1)])))  9.37 us
    pallas_call x4, Pallas kernels, write_out(): pl.pallas_call(kernel, out_shape=shape_of(total, cols, jnp.float32), in_s...  8.51 us
  transfers between devices with their start and end apart: 40, of which 20 were waited for; matrix products, arithmetic and copies ran while one was open for 4% of the time, Pallas kernels for 13%

profile of v4, /device:TPU:1, one launch (start us, length us, event | category | flops | bytes accessed | tf_op | source)
XLA Modules:
  0.0 167.1 jit_solution(3815990111123224021)
XLA Ops:
  3.1 2.2 %collective-permute-start.3 = (bf16[24,4096]{1,0:T(8,128)(2,1)S(1)}, bf16[24,4096]{1,0:T(8,128)(2,1)S(1)}, u32[]{:S(2)}, u32[]{:S(2)}) collective-permute-start(bf16[24,4096]{1,0:T(8,128)(2,1)S(1)} %get-tuple-element.55), channel_id=1, source_target_pairs={{0,2},{2,4},{4,6},{6,0},{8,10},{10,12},{12,14},{14,8},{16,18},{18,... | collective-permute-start | bytes 589832 | tf_op jit(solution)/shard_map/columns_first/ppermute | solution.py:29
  17.1 3.1 %collective-permute-start.8 = (bf16[96,1024]{1,0:T(8,128)(2,1)S(1)}, bf16[96,1024]{1,0:T(8,128)(2,1)S(1)}, u32[]{:S(2)}, u32[]{:S(2)}) collective-permute-start(bf16[96,1024]{1,0:T(8,128)(2,1)S(1)} %get-tuple-element.61), channel_id=1, source_target_pairs={{0,16},{2,18},{4,20},{6,22},{8,24},{10,26},{12,28},{14,30},{16,0},... | collective-permute-start | bytes 589832 | tf_op jit(solution)/shard_map/columns_second/ppermute | solution.py:29
  23.2 3.5 %collective-permute-start.13 = (bf16[384,1024]{1,0:T(8,128)(2,1)S(1)}, bf16[384,1024]{1,0:T(8,128)(2,1)S(1)}, u32[]{:S(2)}, u32[]{:S(2)}) collective-permute-start(bf16[384,1024]{1,0:T(8,128)(2,1)S(1)} %constant_dynamic-update-slice_fusion), channel_id=1, source_target_pairs={{0,65},{1,0},{64,1},{65,64},{2,67},{3,2},{66,3},{67,66},{4,69},{5,... | collective-permute-start | bytes 2359304 | tf_op jit(solution)/shard_map/columns_near/ppermute | solution.py:18
  30.0 10.3 %collective-permute-done.13 = bf16[384,1024]{1,0:T(8,128)(2,1)S(1)} collective-permute-done((bf16[384,1024]{1,0:T(8,128)(2,1)S(1)}, bf16[384,1024]{1,0:T(8,128)(2,1)S(1)}, u32[]{:S(2)}, u32[]{:S(2)}) %collective-permute-start.13) | collective-permute-done | bytes 786464 | tf_op jit(solution)/shard_map/columns_near/ppermute | solution.py:18
  40.3 3.5 %collective-permute-start.17 = (bf16[192,1024]{1,0:T(8,128)(2,1)S(1)}, bf16[192,1024]{1,0:T(8,128)(2,1)S(1)}, u32[]{:S(2)}, u32[]{:S(2)}) collective-permute-start(bf16[192,1024]{1,0:T(8,128)(2,1)S(1)} %slice.41), channel_id=1, source_target_pairs={{0,65},{1,0},{64,1},{65,64},{2,67},{3,2},{66,3},{67,66},{4,69},{5,... | collective-permute-start | bytes 1179656 | tf_op jit(solution)/shard_map/columns_far/ppermute | solution.py:18
  43.8 3.3 %collective-permute-done.10.refs_2_ = bf16[96,4096]{1,0:T(8,128)(2,1)S(1)} collective-permute-done((bf16[96,4096]{1,0:T(8,128)(2,1)S(1)}, bf16[96,4096]{1,0:T(8,128)(2,1)S(1)}, u32[]{:S(2)}, u32[]{:S(2)}) %collective-permute-start.10) | collective-permute-done | bytes 786464 | tf_op jit(solution)/shard_map/panel_ring/ppermute | solution.py:29
  49.8 2.7 %collective-permute-start.21 = (bf16[384,1536]{1,0:T(8,128)(2,1)S(1)}, bf16[384,1536]{1,0:T(8,128)(2,1)S(1)}, u32[]{:S(2)}, u32[]{:S(2)}) collective-permute-start(bf16[384,1536]{1,0:T(8,128)(2,1)S(1)} %get-tuple-element.72.refs_0_), channel_id=1, source_target_pairs={{0,24},{2,26},{4,28},{6,30},{8,0},{10,2},{12,4},{14,6},{16,8},{18,... | collective-permute-start | bytes 3538952 | tf_op jit(solution)/shard_map/near1/ppermute | solution.py:29
  52.6 9.1 %collective-permute-done.16 = bf16[192,1024]{1,0:T(8,128)(2,1)S(1)} collective-permute-done((bf16[192,1024]{1,0:T(8,128)(2,1)S(1)}, bf16[192,1024]{1,0:T(8,128)(2,1)S(1)}, u32[]{:S(2)}, u32[]{:S(2)}) %collective-permute-start.16) | collective-permute-done | bytes 393248 | tf_op jit(solution)/shard_map/columns_far/ppermute | solution.py:18
  62.2 2.8 %collective-permute-start.19 = (bf16[192,1024]{1,0:T(8,128)(2,1)S(1)}, bf16[192,1024]{1,0:T(8,128)(2,1)S(1)}, u32[]{:S(2)}, u32[]{:S(2)}) collective-permute-start(bf16[192,1024]{1,0:T(8,128)(2,1)S(1)} %slice.33), channel_id=1, source_target_pairs={{0,24},{2,26},{4,28},{6,30},{8,0},{10,2},{12,4},{14,6},{16,8},{18,... | collective-permute-start | bytes 1179656 | tf_op jit(solution)/shard_map/far0/ppermute | solution.py:29
  65.0 11.3 %collective-permute-done.19.refs_4_ = bf16[192,1024]{1,0:T(8,128)(2,1)S(1)} collective-permute-done((bf16[192,1024]{1,0:T(8,128)(2,1)S(1)}, bf16[192,1024]{1,0:T(8,128)(2,1)S(1)}, u32[]{:S(2)}, u32[]{:S(2)}) %collective-permute-start.19) | collective-permute-done | bytes 393248 | tf_op jit(solution)/shard_map/far0/ppermute | solution.py:29
  76.3 2.7 %collective-permute-done.18.refs_3_ = bf16[192,1024]{1,0:T(8,128)(2,1)S(1)} collective-permute-done((bf16[192,1024]{1,0:T(8,128)(2,1)S(1)}, bf16[192,1024]{1,0:T(8,128)(2,1)S(1)}, u32[]{:S(2)}, u32[]{:S(2)}) %collective-permute-start.18) | collective-permute-done | bytes 393248 | tf_op jit(solution)/shard_map/far0/ppermute | solution.py:29
  81.2 3.5 %product0.1 = (f32[1024,512]{1,0:T(8,128)S(1)}, bf16[1024,512]{1,0:T(8,128)(2,1)S(1)}) custom-call(bf16[384,1024]{1,0:T(8,128)(2,1)S(1)} %get-tuple-element.67.refs_0_, bf16[384,1024]{1,0:T(8,128)(2,1)S(1)} %collective-permute-done.14.refs_1_, bf16[384,1024]{1,0:T(8,128)(2,1)S(1)} %collective-permute-done.15.refs_2_, ...), custom_call_target="tpu_custom_call" | custom-call | tf_op jit(solution)/shard_map/product0/pallas_call | solution.py:33
  84.6 3.6 %collective-permute-done.23.refs_4_ = bf16[192,1536]{1,0:T(8,128)(2,1)S(1)} collective-permute-done((bf16[192,1536]{1,0:T(8,128)(2,1)S(1)}, bf16[192,1536]{1,0:T(8,128)(2,1)S(1)}, u32[]{:S(2)}, u32[]{:S(2)}) %collective-permute-start.23) | collective-permute-done | bytes 589856 | tf_op jit(solution)/shard_map/far1/ppermute | solution.py:29
  89.7 6.3 %collective-permute-start.24 = (bf16[1024,512]{1,0:T(8,128)(2,1)S(1)}, bf16[1024,512]{1,0:T(8,128)(2,1)S(1)}, u32[]{:S(2)}, u32[]{:S(2)}) collective-permute-start(bf16[1024,512]{1,0:T(8,128)(2,1)S(1)} %get-tuple-element.75), channel_id=1, source_target_pairs={{0,32},{32,0},{1,33},{33,1},{2,34},{34,2},{3,35},{35,3},{4,36},{36... | collective-permute-start | bytes 3145736 | tf_op jit(solution)/shard_map/exchange0/ppermute | solution.py:125
  101.9 2.2 %collective-permute-start.30 = (bf16[384,512]{1,0:T(8,128)(2,1)S(1)}, bf16[384,512]{1,0:T(8,128)(2,1)S(1)}, u32[]{:S(2)}, u32[]{:S(2)}) collective-permute-start(bf16[384,512]{1,0:T(8,128)(2,1)S(1)} %get-tuple-element.83.refs_0_), channel_id=1, source_target_pairs={{0,24},{2,26},{4,28},{6,30},{8,0},{10,2},{12,4},{14,6},{16,8},{18,... | collective-permute-start | bytes 1179656 | tf_op jit(solution)/shard_map/near3/ppermute | solution.py:29
  104.1 3.0 %collective-permute-done.26.refs_2_ = bf16[384,1024]{1,0:T(8,128)(2,1)S(1)} collective-permute-done((bf16[384,1024]{1,0:T(8,128)(2,1)S(1)}, bf16[384,1024]{1,0:T(8,128)(2,1)S(1)}, u32[]{:S(2)}, u32[]{:S(2)}) %collective-permute-start.26) | collective-permute-done | bytes 786464 | tf_op jit(solution)/shard_map/near2/ppermute | solution.py:29
  107.1 2.9 %collective-permute-done.25.refs_1_ = bf16[384,1024]{1,0:T(8,128)(2,1)S(1)} collective-permute-done((bf16[384,1024]{1,0:T(8,128)(2,1)S(1)}, bf16[384,1024]{1,0:T(8,128)(2,1)S(1)}, u32[]{:S(2)}, u32[]{:S(2)}) %collective-permute-start.25) | collective-permute-done | bytes 786464 | tf_op jit(solution)/shard_map/near2/ppermute | solution.py:29
  111.7 5.1 %product1.1 = (f32[1536,512]{1,0:T(8,128)S(1)}, bf16[1536,512]{1,0:T(8,128)(2,1)S(1)}) custom-call(bf16[384,1536]{1,0:T(8,128)(2,1)S(1)} %get-tuple-element.72.refs_0_, bf16[384,1536]{1,0:T(8,128)(2,1)S(1)} %collective-permute-done.20.refs_1_, bf16[384,1536]{1,0:T(8,128)(2,1)S(1)} %collective-permute-done.21.refs_2_, ...), custom_call_target="tpu_custom_call" | custom-call | tf_op jit(solution)/shard_map/product1/pallas_call | solution.py:33
  120.3 3.5 %product2.1 = (f32[1024,512]{1,0:T(8,128)S(1)}, bf16[1024,512]{1,0:T(8,128)(2,1)S(1)}) custom-call(bf16[384,1024]{1,0:T(8,128)(2,1)S(1)} %get-tuple-element.79.refs_0_, bf16[384,1024]{1,0:T(8,128)(2,1)S(1)} %collective-permute-done.25.refs_1_, bf16[384,1024]{1,0:T(8,128)(2,1)S(1)} %collective-permute-done.26.refs_2_, ...), custom_call_target="tpu_custom_call" | custom-call | tf_op jit(solution)/shard_map/product2/pallas_call | solution.py:33
  131.9 3.6 %collective-permute-start.39 = (bf16[1024,512]{1,0:T(8,128)(2,1)}, bf16[1024,512]{1,0:T(8,128)(2,1)}, u32[]{:S(2)}, u32[]{:S(2)}) collective-permute-start(bf16[1024,512]{1,0:T(8,128)(2,1)} %get-tuple-element.97), channel_id=1, source_target_pairs={{1,32},{32,1},{3,34},{34,3},{5,36},{36,5},{7,38},{38,7},{9,40},{40... | collective-permute-start | bytes 3145736 | tf_op jit(solution)/shard_map/swap2/ppermute | solution.py:225
  137.0 10.8 %collective-permute-done.37.moved_ref = bf16[1536,512]{1,0:T(8,128)(2,1)S(1)} collective-permute-done((bf16[1536,512]{1,0:T(8,128)(2,1)S(1)}, bf16[1536,512]{1,0:T(8,128)(2,1)S(1)}, u32[]{:S(2)}, u32[]{:S(2)}) %collective-permute-start.37) | collective-permute-done | bytes 1572896 | tf_op jit(solution)/shard_map/swap1/ppermute | solution.py:225
  159.2 2.9 %shard_map.41.refs_0_ = f32[4096,512]{1,0:T(8,128)} custom-call(s32[1]{0:T(128)} %bitcast.stays_ref, f32[1024,512]{1,0:T(8,128)S(1)} %copy-done.1, bf16[1024,512]{1,0:T(8,128)(2,1)} %collective-permute-done.39.moved_ref, f32[4096,512]{1,0:T(8,128)} %shard_map.40.refs_0_), custom_call_target="tpu_custom_call", output_to_operand_aliasing={{}: (3, {})} | custom-call | tf_op jit(solution)/shard_map/pallas_call | solution.py:139
  162.1 2.7 %collective-permute-done.38.moved_ref = bf16[512,512]{1,0:T(8,128)(2,1)} collective-permute-done((bf16[512,512]{1,0:T(8,128)(2,1)}, bf16[512,512]{1,0:T(8,128)(2,1)}, u32[]{:S(2)}, u32[]{:S(2)}) %collective-permute-start.38) | collective-permute-done | bytes 524320 | tf_op jit(solution)/shard_map/swap3/ppermute | solution.py:225
  164.8 2.1 %shard_map.42 = f32[4096,512]{1,0:T(8,128)} custom-call(s32[1]{0:T(128)} %bitcast.stays_ref, f32[512,512]{1,0:T(8,128)S(1)} %copy-done.2, bf16[512,512]{1,0:T(8,128)(2,1)} %collective-permute-done.38.moved_ref, f32[4096,512]{1,0:T(8,128)} %shard_map.41.refs_0_), custom_call_target="tpu_custom_call", output_to_operand_aliasing={{}: (3, {})} | custom-call | tf_op jit(solution)/shard_map/pallas_call | solution.py:139
  (108 shorter events, 60.0 us)
Async XLA Ops:
  10.1 10.1 %collective-permute-start.1 = (bf16[24,4096]{1,0:T(8,128)(2,1)S(1)}, bf16[24,4096]{1,0:T(8,128)(2,1)S(1)}, u32[]{:S(2)}, u32[]{:S(2)}) collective-permute-start(bf16[24,4096]{1,0:T(8,128)(2,1)S(1)} %get-tuple-element.52), channel_id=1, source_target_pairs={{0,65},{1,0},{64,1},{65,64},{2,67},{3,2},{66,3},{67,66},{4,69},{5,... | collective-permute-start | bytes 589832 | tf_op jit(solution)/shard_map/panel_z/ppermute | solution.py:18
  23.2 17.0 %collective-permute-start.13 = (bf16[384,1024]{1,0:T(8,128)(2,1)S(1)}, bf16[384,1024]{1,0:T(8,128)(2,1)S(1)}, u32[]{:S(2)}, u32[]{:S(2)}) collective-permute-start(bf16[384,1024]{1,0:T(8,128)(2,1)S(1)} %constant_dynamic-update-slice_fusion), channel_id=1, source_target_pairs={{0,65},{1,0},{64,1},{65,64},{2,67},{3,2},{66,3},{67,66},{4,69},{5,... | collective-permute-start | bytes 2359304 | tf_op jit(solution)/shard_map/columns_near/ppermute | solution.py:18
  26.8 17.0 %collective-permute-start.11 = (bf16[96,4096]{1,0:T(8,128)(2,1)S(1)}, bf16[96,4096]{1,0:T(8,128)(2,1)S(1)}, u32[]{:S(2)}, u32[]{:S(2)}) collective-permute-start(bf16[96,4096]{1,0:T(8,128)(2,1)S(1)} %pad_maximum_fusion.1.refs_0_), channel_id=1, source_target_pairs={{0,4},{2,6},{4,0},{6,2},{8,12},{10,14},{12,8},{14,10},{16,20},{18,... | collective-permute-start | bytes 2359304 | tf_op jit(solution)/shard_map/panel_ring/ppermute | solution.py:29
  28.1 19.0 %collective-permute-start.10 = (bf16[96,4096]{1,0:T(8,128)(2,1)S(1)}, bf16[96,4096]{1,0:T(8,128)(2,1)S(1)}, u32[]{:S(2)}, u32[]{:S(2)}) collective-permute-start(bf16[96,4096]{1,0:T(8,128)(2,1)S(1)} %pad_maximum_fusion.1.refs_0_), channel_id=1, source_target_pairs={{0,6},{2,0},{4,2},{6,4},{8,14},{10,8},{12,10},{14,12},{16,22},{18,... | collective-permute-start | bytes 2359304 | tf_op jit(solution)/shard_map/panel_ring/ppermute | solution.py:29
  30.0 17.8 %collective-permute-start.9 = (bf16[96,4096]{1,0:T(8,128)(2,1)S(1)}, bf16[96,4096]{1,0:T(8,128)(2,1)S(1)}, u32[]{:S(2)}, u32[]{:S(2)}) collective-permute-start(bf16[96,4096]{1,0:T(8,128)(2,1)S(1)} %pad_maximum_fusion.1.refs_0_), channel_id=1, source_target_pairs={{0,2},{2,4},{4,6},{6,0},{8,10},{10,12},{12,14},{14,8},{16,18},{18,... | collective-permute-start | bytes 2359304 | tf_op jit(solution)/shard_map/panel_ring/ppermute | solution.py:29
  30.0 17.8 %collective-permute-start.12 = (bf16[384,1024]{1,0:T(8,128)(2,1)S(1)}, bf16[384,1024]{1,0:T(8,128)(2,1)S(1)}, u32[]{:S(2)}, u32[]{:S(2)}) collective-permute-start(bf16[384,1024]{1,0:T(8,128)(2,1)S(1)} %constant_dynamic-update-slice_fusion), channel_id=1, source_target_pairs={{0,1},{1,64},{64,65},{65,0},{2,3},{3,66},{66,67},{67,2},{4,5},{5,6... | collective-permute-start | bytes 2359304 | tf_op jit(solution)/shard_map/columns_near/ppermute | solution.py:18
  40.3 12.2 %collective-permute-start.17 = (bf16[192,1024]{1,0:T(8,128)(2,1)S(1)}, bf16[192,1024]{1,0:T(8,128)(2,1)S(1)}, u32[]{:S(2)}, u32[]{:S(2)}) collective-permute-start(bf16[192,1024]{1,0:T(8,128)(2,1)S(1)} %slice.41), channel_id=1, source_target_pairs={{0,65},{1,0},{64,1},{65,64},{2,67},{3,2},{66,3},{67,66},{4,69},{5,... | collective-permute-start | bytes 1179656 | tf_op jit(solution)/shard_map/columns_far/ppermute | solution.py:18
  48.0 13.7 %collective-permute-start.15 = (bf16[384,1024]{1,0:T(8,128)(2,1)S(1)}, bf16[384,1024]{1,0:T(8,128)(2,1)S(1)}, u32[]{:S(2)}, u32[]{:S(2)}) collective-permute-start(bf16[384,1024]{1,0:T(8,128)(2,1)S(1)} %get-tuple-element.67.refs_0_), channel_id=1, source_target_pairs={{0,24},{2,26},{4,28},{6,30},{8,0},{10,2},{12,4},{14,6},{16,8},{18,... | collective-permute-start | bytes 2359304 | tf_op jit(solution)/shard_map/near0/ppermute | solution.py:29
  49.8 12.3 %collective-permute-start.14 = (bf16[384,1024]{1,0:T(8,128)(2,1)S(1)}, bf16[384,1024]{1,0:T(8,128)(2,1)S(1)}, u32[]{:S(2)}, u32[]{:S(2)}) collective-permute-start(bf16[384,1024]{1,0:T(8,128)(2,1)S(1)} %get-tuple-element.67.refs_0_), channel_id=1, source_target_pairs={{0,8},{2,10},{4,12},{6,14},{8,16},{10,18},{12,20},{14,22},{16,24},... | collective-permute-start | bytes 2359304 | tf_op jit(solution)/shard_map/near0/ppermute | solution.py:29
  49.8 29.2 %collective-permute-start.21 = (bf16[384,1536]{1,0:T(8,128)(2,1)S(1)}, bf16[384,1536]{1,0:T(8,128)(2,1)S(1)}, u32[]{:S(2)}, u32[]{:S(2)}) collective-permute-start(bf16[384,1536]{1,0:T(8,128)(2,1)S(1)} %get-tuple-element.72.refs_0_), channel_id=1, source_target_pairs={{0,24},{2,26},{4,28},{6,30},{8,0},{10,2},{12,4},{14,6},{16,8},{18,... | collective-permute-start | bytes 3538952 | tf_op jit(solution)/shard_map/near1/ppermute | solution.py:29
  52.5 26.5 %collective-permute-start.20 = (bf16[384,1536]{1,0:T(8,128)(2,1)S(1)}, bf16[384,1536]{1,0:T(8,128)(2,1)S(1)}, u32[]{:S(2)}, u32[]{:S(2)}) collective-permute-start(bf16[384,1536]{1,0:T(8,128)(2,1)S(1)} %get-tuple-element.72.refs_0_), channel_id=1, source_target_pairs={{0,8},{2,10},{4,12},{6,14},{8,16},{10,18},{12,20},{14,22},{16,24},... | collective-permute-start | bytes 3538952 | tf_op jit(solution)/shard_map/near1/ppermute | solution.py:29
  52.6 9.2 %collective-permute-start.16 = (bf16[192,1024]{1,0:T(8,128)(2,1)S(1)}, bf16[192,1024]{1,0:T(8,128)(2,1)S(1)}, u32[]{:S(2)}, u32[]{:S(2)}) collective-permute-start(bf16[192,1024]{1,0:T(8,128)(2,1)S(1)} %slice.40), channel_id=1, source_target_pairs={{0,1},{1,64},{64,65},{65,0},{2,3},{3,66},{66,67},{67,2},{4,5},{5,6... | collective-permute-start | bytes 1179656 | tf_op jit(solution)/shard_map/columns_far/ppermute | solution.py:18
  62.2 14.1 %collective-permute-start.19 = (bf16[192,1024]{1,0:T(8,128)(2,1)S(1)}, bf16[192,1024]{1,0:T(8,128)(2,1)S(1)}, u32[]{:S(2)}, u32[]{:S(2)}) collective-permute-start(bf16[192,1024]{1,0:T(8,128)(2,1)S(1)} %slice.33), channel_id=1, source_target_pairs={{0,24},{2,26},{4,28},{6,30},{8,0},{10,2},{12,4},{14,6},{16,8},{18,... | collective-permute-start | bytes 1179656 | tf_op jit(solution)/shard_map/far0/ppermute | solution.py:29
  65.0 14.0 %collective-permute-start.18 = (bf16[192,1024]{1,0:T(8,128)(2,1)S(1)}, bf16[192,1024]{1,0:T(8,128)(2,1)S(1)}, u32[]{:S(2)}, u32[]{:S(2)}) collective-permute-start(bf16[192,1024]{1,0:T(8,128)(2,1)S(1)} %slice.32), channel_id=1, source_target_pairs={{0,8},{2,10},{4,12},{6,14},{8,16},{10,18},{12,20},{14,22},{16,24},... | collective-permute-start | bytes 1179656 | tf_op jit(solution)/shard_map/far0/ppermute | solution.py:29
  79.1 9.1 %collective-permute-start.23 = (bf16[192,1536]{1,0:T(8,128)(2,1)S(1)}, bf16[192,1536]{1,0:T(8,128)(2,1)S(1)}, u32[]{:S(2)}, u32[]{:S(2)}) collective-permute-start(bf16[192,1536]{1,0:T(8,128)(2,1)S(1)} %slice.35), channel_id=1, source_target_pairs={{0,24},{2,26},{4,28},{6,30},{8,0},{10,2},{12,4},{14,6},{16,8},{18,... | collective-permute-start | bytes 1769480 | tf_op jit(solution)/shard_map/far1/ppermute | solution.py:29
  79.2 10.5 %collective-permute-start.22 = (bf16[192,1536]{1,0:T(8,128)(2,1)S(1)}, bf16[192,1536]{1,0:T(8,128)(2,1)S(1)}, u32[]{:S(2)}, u32[]{:S(2)}) collective-permute-start(bf16[192,1536]{1,0:T(8,128)(2,1)S(1)} %slice.34), channel_id=1, source_target_pairs={{0,8},{2,10},{4,12},{6,14},{8,16},{10,18},{12,20},{14,22},{16,24},... | collective-permute-start | bytes 1769480 | tf_op jit(solution)/shard_map/far1/ppermute | solution.py:29
  96.0 11.1 %collective-permute-start.26 = (bf16[384,1024]{1,0:T(8,128)(2,1)S(1)}, bf16[384,1024]{1,0:T(8,128)(2,1)S(1)}, u32[]{:S(2)}, u32[]{:S(2)}) collective-permute-start(bf16[384,1024]{1,0:T(8,128)(2,1)S(1)} %get-tuple-element.79.refs_0_), channel_id=1, source_target_pairs={{0,24},{2,26},{4,28},{6,30},{8,0},{10,2},{12,4},{14,6},{16,8},{18,... | collective-permute-start | bytes 2359304 | tf_op jit(solution)/shard_map/near2/ppermute | solution.py:29
  97.7 12.3 %collective-permute-start.25 = (bf16[384,1024]{1,0:T(8,128)(2,1)S(1)}, bf16[384,1024]{1,0:T(8,128)(2,1)S(1)}, u32[]{:S(2)}, u32[]{:S(2)}) collective-permute-start(bf16[384,1024]{1,0:T(8,128)(2,1)S(1)} %get-tuple-element.79.refs_0_), channel_id=1, source_target_pairs={{0,8},{2,10},{4,12},{6,14},{8,16},{10,18},{12,20},{14,22},{16,24},... | collective-permute-start | bytes 2359304 | tf_op jit(solution)/shard_map/near2/ppermute | solution.py:29
  100.0 18.2 %collective-permute-start.31 = (bf16[1024,512]{1,0:T(8,128)(2,1)S(1)}, bf16[1024,512]{1,0:T(8,128)(2,1)S(1)}, u32[]{:S(2)}, u32[]{:S(2)}) collective-permute-start(bf16[1024,512]{1,0:T(8,128)(2,1)S(1)} %get-tuple-element.101), channel_id=1, source_target_pairs={{1,32},{32,1},{3,34},{34,3},{5,36},{36,5},{7,38},{38,7},{9,40},{40... | collective-permute-start | bytes 3145736 | tf_op jit(solution)/shard_map/swap0/ppermute | solution.py:225
  101.9 14.8 %collective-permute-start.30 = (bf16[384,512]{1,0:T(8,128)(2,1)S(1)}, bf16[384,512]{1,0:T(8,128)(2,1)S(1)}, u32[]{:S(2)}, u32[]{:S(2)}) collective-permute-start(bf16[384,512]{1,0:T(8,128)(2,1)S(1)} %get-tuple-element.83.refs_0_), channel_id=1, source_target_pairs={{0,24},{2,26},{4,28},{6,30},{8,0},{10,2},{12,4},{14,6},{16,8},{18,... | collective-permute-start | bytes 1179656 | tf_op jit(solution)/shard_map/near3/ppermute | solution.py:29
  104.1 12.7 %collective-permute-start.29 = (bf16[384,512]{1,0:T(8,128)(2,1)S(1)}, bf16[384,512]{1,0:T(8,128)(2,1)S(1)}, u32[]{:S(2)}, u32[]{:S(2)}) collective-permute-start(bf16[384,512]{1,0:T(8,128)(2,1)S(1)} %get-tuple-element.83.refs_0_), channel_id=1, source_target_pairs={{0,8},{2,10},{4,12},{6,14},{8,16},{10,18},{12,20},{14,22},{16,24},... | collective-permute-start | bytes 1179656 | tf_op jit(solution)/shard_map/near3/ppermute | solution.py:29
  126.1 21.7 %collective-permute-start.37 = (bf16[1536,512]{1,0:T(8,128)(2,1)S(1)}, bf16[1536,512]{1,0:T(8,128)(2,1)S(1)}, u32[]{:S(2)}, u32[]{:S(2)}) collective-permute-start(bf16[1536,512]{1,0:T(8,128)(2,1)S(1)} %get-tuple-element.99), channel_id=1, source_target_pairs={{1,32},{32,1},{3,34},{34,3},{5,36},{36,5},{7,38},{38,7},{9,40},{40... | collective-permute-start | bytes 4718600 | tf_op jit(solution)/shard_map/swap1/ppermute | solution.py:225
  131.9 27.3 %collective-permute-start.39 = (bf16[1024,512]{1,0:T(8,128)(2,1)}, bf16[1024,512]{1,0:T(8,128)(2,1)}, u32[]{:S(2)}, u32[]{:S(2)}) collective-permute-start(bf16[1024,512]{1,0:T(8,128)(2,1)} %get-tuple-element.97), channel_id=1, source_target_pairs={{1,32},{32,1},{3,34},{34,3},{5,36},{36,5},{7,38},{38,7},{9,40},{40... | collective-permute-start | bytes 3145736 | tf_op jit(solution)/shard_map/swap2/ppermute | solution.py:225
  149.0 15.8 %collective-permute-start.38 = (bf16[512,512]{1,0:T(8,128)(2,1)}, bf16[512,512]{1,0:T(8,128)(2,1)}, u32[]{:S(2)}, u32[]{:S(2)}) collective-permute-start(bf16[512,512]{1,0:T(8,128)(2,1)} %get-tuple-element.93), channel_id=1, source_target_pairs={{1,32},{32,1},{3,34},{34,3},{5,36},{36,5},{7,38},{38,7},{9,40},{40... | collective-permute-start | bytes 1572872 | tf_op jit(solution)/shard_map/swap3/ppermute | solution.py:225
  (24 other events, 130.8 us)
